TPU v7x, 32 devices: a whole 2x2x4 slice. The times are simulated.
32 devices in a mesh: groups: 2 (over y), context: 8 (over z, x), tensor: 2 (over core).
Axes of the slice: x: 2, y: 2, z: 4, core: 2. Of those that a mesh axis runs over, the one named last changes fastest.
Arguments:
- q_raw: bfloat16 [2048, 1024], P(('groups', 'context'), 'tensor'), parts along dimension 0, may hold values from -6 to 6
- k_raw: bfloat16 [2048, 1024], P(('groups', 'context'), 'tensor'), parts along dimension 0, may hold values from -6 to 6
- v_raw: bfloat16 [2048, 2048], P(('groups', 'context'), 'tensor'), parts along dimension 0, may hold values from -6 to 6
- gate_z: bfloat16 [2048, 2048], P(('groups', 'context'), 'tensor'), parts along dimension 0, may hold values from -6 to 6
- beta_logit: float32 [2048, 16], P(('groups', 'context'), 'tensor'), parts along dimension 0
- decay_in: float32 [2048, 16], P(('groups', 'context'), 'tensor'), parts along dimension 0
- conv_q: bfloat16 [4, 1024], P(None, 'tensor'), may hold values from -3 to 3
- conv_k: bfloat16 [4, 1024], P(None, 'tensor'), may hold values from -3 to 3
- conv_v: bfloat16 [4, 2048], P(None, 'tensor'), may hold values from -3 to 3
- a_log: float32 [16], P('tensor'), may hold values from 0 to 1.1
- dt_bias: float32 [16], P('tensor'), may hold values from -0.5 to 0.5
- norm_gain: float32 [128], replicated, may hold values from 0.25 to 1.75
Outputs:
- mixed_out: bfloat16 [2048, 2048], P(('groups', 'context'), 'tensor'), parts along dimension 0
There are 2 independent parts, one for each index of `groups`. A program takes and returns all parts, laid end to end along the dimension named above; an argument that names none is the same for every part. Nothing has to cross between parts.
All inputs are finite; a program needn't handle non-finite values.
Results may differ from a plain program's by a relative error of at most 0.0085.
Values may be sent and summed in bfloat16 or wider, within the bound.
A program may use at most 256 MiB of HBM per device.

v0:
```python
from functools import partial

import jax
import jax.numpy as jnp
from jax import lax
from jax.sharding import PartitionSpec as P

SPAN = 64


HIGH = lax.Precision.HIGHEST


def passed_along(block, axis, distance):
    devices = range(lax.axis_size(axis))
    route = [(i - distance, i) for i in devices if i - distance in devices]
    return lax.ppermute(block, axis, route)


def carried_in(part, axis, combine, identity):
    place = lax.axis_index(axis)
    gathered = jax.tree.map(lambda a: lax.all_gather(a, axis), part)
    state = jax.tree.map(lambda a, e: jnp.zeros_like(a) + jnp.asarray(e, a.dtype), part, identity)

    def one(turn, state):
        return combine(
            state, jax.tree.map(lambda a: lax.dynamic_index_in_dim(a, turn, 0, False), gathered)
        )

    return lax.fori_loop(0, place, one, state)


def mixing_weight(form, left, right):
    return jnp.einsum(form, left, right, precision=HIGH)


def causal_conv(rows, rim, weights):
    full = jnp.concatenate([rim, rows], axis=0).astype(jnp.float32)
    taps = weights.shape[0]
    count = rows.shape[0]
    total = jnp.zeros((count, rows.shape[1]), jnp.float32)
    for place in range(taps):
        total = total + weights[place].astype(jnp.float32)[None, :] * full[place : place + count]
    return jax.nn.silu(total).astype(jnp.bfloat16)


def prepare(query_rows, key_rows, value_rows, beta_logit, decay_in, a_log, dt_bias, size):
    rows = query_rows.shape[0]
    kheads = query_rows.shape[1] // size
    vheads = value_rows.shape[1] // size
    repeat = vheads // kheads

    def unit(block):
        block = block.astype(jnp.float32).reshape(rows, kheads, size)
        block = block / jnp.sqrt(jnp.sum(block * block, axis=-1, keepdims=True) + 1e-06)
        return jnp.repeat(block, repeat, axis=1)

    q_unit = unit(query_rows) * size ** (-0.5)
    k_unit = unit(key_rows)
    v_full = value_rows.astype(jnp.float32).reshape(rows, vheads, size)
    betas = jax.nn.sigmoid(beta_logit)
    decays = -jnp.exp(a_log)[None, :] * jax.nn.softplus(decay_in + dt_bias[None, :])
    return (q_unit, k_unit, v_full, betas, decays)


def to_blocks(array, span):
    count = array.shape[0] // span
    array = array.reshape((count, span) + array.shape[1:])
    return jnp.swapaxes(array, 1, 2)


def unpack_segments(array):
    array = jnp.swapaxes(array, 1, 2)
    return array.reshape((array.shape[0] * array.shape[1],) + array.shape[2:])


def span_parts(query_rows, key_rows, betas, decays):
    count = decays.shape[-1]
    cumul = jnp.cumsum(decays, axis=-1)
    place = jnp.arange(count)
    later = place[:, None] >= place[None, :]
    strict = place[:, None] > place[None, :]
    gap = cumul[:, :, None] - cumul[:, None, :]
    ratio = jnp.where(later[None], jnp.exp(jnp.minimum(gap, 0.0)), 0.0)
    inner = mixing_weight("hck,hdk->hcd", key_rows, key_rows)
    lower = jnp.where(strict[None], betas[:, :, None] * ratio * inner, 0.0)
    system = lower + jnp.eye(count, dtype=jnp.float32)[None]
    score_matrix = mixing_weight("hck,hdk->hcd", query_rows, key_rows) * ratio
    growth_factor = jnp.exp(cumul)
    tail_tokens = jnp.exp(cumul[:, -1:] - cumul)
    return (system, score_matrix, growth_factor, tail_tokens)


def solve_lower(system, rhs):
    count = system.shape[-1]
    unit_matrix = jnp.eye(count, dtype=system.dtype)[None]
    power = unit_matrix - system
    inverse = unit_matrix + power
    levels = (count - 1).bit_length()
    for level in range(1, levels):
        power = mixing_weight("hij,hjk->hik", power, power)
        inverse = inverse + mixing_weight("hij,hjk->hik", inverse, power)
    return mixing_weight("hij,hjk->hik", inverse, rhs)


def span_apply(state_matrix, inputs):
    query_rows, key_rows, value_rows, betas, decays = inputs
    system, score_matrix, growth_factor, tail_tokens = span_parts(
        query_rows, key_rows, betas, decays
    )
    known_prefix = value_rows - growth_factor[:, :, None] * mixing_weight(
        "uxz,uzn->uxn", key_rows, state_matrix
    )
    state_update = solve_lower(system, betas[:, :, None] * known_prefix)
    output_rows = growth_factor[:, :, None] * mixing_weight(
        "uxz,uzn->uxn", query_rows, state_matrix
    ) + mixing_weight("jpr,jrf->jpf", score_matrix, state_update)
    last_token = growth_factor[:, -1][:, None, None]
    updated_state = last_token * state_matrix + mixing_weight(
        "rbe,rbi->rei", key_rows, tail_tokens[:, :, None] * state_update
    )
    return (updated_state, output_rows)


def affine_step(with_outputs, carry, inputs):
    trans, base_offset = carry
    query_rows, key_rows, value_rows, betas, decays = inputs
    vsize = value_rows.shape[-1]
    ksize = key_rows.shape[-1]
    system, score_matrix, growth_factor, tail_tokens = span_parts(
        query_rows, key_rows, betas, decays
    )
    known_prefix = value_rows - growth_factor[:, :, None] * mixing_weight(
        "uxz,uzn->uxn", key_rows, base_offset
    )
    rhs = jnp.concatenate(
        [betas[:, :, None] * known_prefix, (betas * growth_factor)[:, :, None] * key_rows], axis=-1
    )
    solved = solve_lower(system, rhs)
    state_update = solved[:, :, :vsize]
    folded = solved[:, :, vsize:]
    last_token = growth_factor[:, -1][:, None, None]
    updated_offset = last_token * base_offset + mixing_weight(
        "rbe,rbi->rei", key_rows, tail_tokens[:, :, None] * state_update
    )
    shrink = last_token * jnp.eye(ksize, dtype=jnp.float32)[None] - mixing_weight(
        "hck,hcj->hkj", key_rows, tail_tokens[:, :, None] * folded
    )
    fresh_transition_map = mixing_weight("hkj,hjl->hkl", shrink, trans)
    return ((fresh_transition_map, updated_offset), None)


def compose(earlier, later):
    trans = mixing_weight("hij,hjk->hik", later[0], earlier[0])
    base_offset = mixing_weight("hij,hjk->hik", later[0], earlier[1]) + later[1]
    return (trans, base_offset)


def finish(mixed, gate_z, norm_gain):
    rows = mixed.shape[0]
    scale = jnp.sqrt(jnp.mean(mixed * mixed, axis=-1, keepdims=True) + 1e-06)
    gate = gate_z.astype(jnp.float32).reshape(mixed.shape)
    result = mixed / scale * norm_gain[None, None, :] * jax.nn.silu(gate)
    return result.reshape(rows, -1).astype(jnp.bfloat16)


def per_device(
    q_raw,
    k_raw,
    v_raw,
    gate_z,
    beta_logit,
    decay_in,
    conv_q,
    conv_k,
    conv_v,
    a_log,
    dt_bias,
    norm_gain,
):
    size = norm_gain.shape[0]
    taps = conv_q.shape[0]
    rows = q_raw.shape[0]
    width_q = q_raw.shape[1]
    edge = jnp.concatenate(
        [q_raw[rows - taps + 1 :], k_raw[rows - taps + 1 :], v_raw[rows - taps + 1 :]], axis=1
    )
    before = passed_along(edge, "context", 1)
    query_rows = causal_conv(q_raw, before[:, :width_q], conv_q)
    key_rows = causal_conv(k_raw, before[:, width_q : 2 * width_q], conv_k)
    value_rows = causal_conv(v_raw, before[:, 2 * width_q :], conv_v)
    prepared = prepare(query_rows, key_rows, value_rows, beta_logit, decay_in, a_log, dt_bias, size)
    inputs = tuple((to_blocks(array, SPAN) for array in prepared))
    heads = prepared[2].shape[1]
    identity = (
        jnp.broadcast_to(jnp.eye(size, dtype=jnp.float32), (heads, size, size)),
        jnp.zeros((heads, size, size), jnp.float32),
    )
    summary, pieces = lax.scan(partial(affine_step, False), identity, inputs)
    prefix = carried_in(summary, "context", compose, identity)
    final, mixer_results = lax.scan(span_apply, prefix[1], inputs)
    return finish(unpack_segments(mixer_results), gate_z, norm_gain)


def solution(mesh):
    return jax.shard_map(
        per_device,
        mesh=mesh,
        in_specs=(
            P(("groups", "context"), "tensor"),
            P(("groups", "context"), "tensor"),
            P(("groups", "context"), "tensor"),
            P(("groups", "context"), "tensor"),
            P(("groups", "context"), "tensor"),
            P(("groups", "context"), "tensor"),
            P(None, "tensor"),
            P(None, "tensor"),
            P(None, "tensor"),
            P("tensor"),
            P("tensor"),
            P(),
        ),
        out_specs=P(("groups", "context"), "tensor"),
        check_vma=False,
    )
```

profile of v0, /device:TPU:26, one launch (start us, length us, event | category | flops | bytes accessed | tf_op | source)
XLA Modules:
  0.0 224.8 jit_solution(1904706812610185726)
XLA Ops:
  6.5 0.8 slice.115
  7.3 0.7 slice.113
  8.0 0.7 slice.114
  8.8 1.3 collective-permute-start
  10.1 0.8 slice_convert_fusion.11
  10.9 0.9 slice_convert_fusion.3
  11.8 0.7 exponential_negate_fusion
  12.4 0.7 add_divide_fusion
  13.1 0.8 fusion.82
  14.4 1.0 maximum_convert_fusion.1
  17.0 19.3 %while.39 = (s32[]{:T(128)}, f32[8,128,128]{2,1,0:T(8,128)S(1)}, f32[8,128,128]{2,1,0:T(8,128)S(1)}, f32[2,8,64]{2,1,0:T(8,128)S(1)}, f32[2,8,64,128]{3,2,1,0:T(...) while((s32[]{:T(128)}, f32[8,128,128]{2,1,0:T(8,128)S(1)}, ...), condition=%wide.region_3.4_spmd.clone, body=%wide.region_1.3_spmd.clone.sunk | while | flops 907821568 | bytes 12202284 | solution.py:199
  17.5 0.6 fusion.304
  18.5 0.4 convolution_add_fusion.34
  19.3 0.4 convolution_add_fusion.35
  20.9 0.4 convolution_add_fusion.37
  21.7 0.4 convolution_add_fusion.38
  22.1 0.6 fusion.310
  22.8 0.6 fusion.311
  23.6 1.1 convolution_subtract_fusion.2
  24.8 0.7 fusion.313
  25.5 1.2 convolution_add_fusion.39
  27.2 0.6 fusion.304
  28.2 0.4 convolution_add_fusion.34
  30.6 0.4 convolution_add_fusion.37
  31.4 0.4 convolution_add_fusion.38
  31.8 0.6 fusion.310
  32.5 0.6 fusion.311
  33.3 1.1 convolution_subtract_fusion.2
  34.5 0.7 fusion.313
  35.1 1.2 convolution_add_fusion.39
  36.4 0.8 copy-done.2
  37.4 0.5 all-gather.7.cloned.1.call-update
  38.8 71.2 %all-gather.5.cloned.1.call-done = f32[64,128,128]{2,1,0:T(8,128)} async-done(((f32[8,128,128]{2,1,0:T(8,128)}), f32[64,128,128]{2,1,0:T(8,128)}) %all-gather.5.cloned.1.call-update) | async-done | bytes 4194320 | tf_op jit(solution)/shard_map/all_gather | solution.py:22
  110.0 73.8 %all-gather.7.cloned.1.call-done = f32[64,128,128]{2,1,0:T(8,128)} async-done(((f32[8,128,128]{2,1,0:T(8,128)}), f32[64,128,128]{2,1,0:T(8,128)}) %all-gather.7.cloned.1.call-update) | async-done | bytes 4194320 | tf_op jit(solution)/shard_map/all_gather | solution.py:22
  183.8 13.9 %while.37 = (s32[]{:T(128)}, f32[8,128,128]{2,1,0:T(8,128)S(1)}, s32[]{:T(128)}, f32[8,8,128,128]{3,2,1,0:T(8,128)}, f32[8,8,128,128]{3,2,1,0:T(8,128)}, /*index=5*/s32[]{:T(128)}, s32[]{:T(128)}, s32[]{:T(128)}) while((s32[]{:T(128)}, f32[8,128,128]{2,1,0:T(8,128)S(1)}, s32[]{:T(128)}, f32[8,8,128,128]{3,2,1,0:T(8,128)}, ...), condition=%wide.region_5.6_spmd, body=%wide.region_4.5_spmd.sunk | while | flops 201457664 | bytes 3146871 | solution.py:30
  184.1 1.9 convolution_add_fusion.27
  186.0 1.9 convolution_add_fusion.27
  188.0 1.9 convolution_add_fusion.27
  190.0 1.9 convolution_add_fusion.27
  191.9 1.9 convolution_add_fusion.27
  193.9 1.9 convolution_add_fusion.27
  195.9 1.9 convolution_add_fusion.27
  197.8 18.2 %while.38 = (s32[]{:T(128)}, f32[8,128,128]{2,1,0:T(8,128)S(1)}, f32[2,8,64,128]{3,2,1,0:T(8,128)S(1)}, f32[2,8,64]{2,1,0:T(8,128)S(1)}, f32[2,8,64,128]{3,2,1,0...) while((s32[]{:T(128)}, f32[8,128,128]{2,1,0:T(8,128)S(1)}, ...), condition=%wide.region_9.10_spmd, body=%wide.region_7.9_spmd.sunk | while | flops 756269056 | bytes 10117917 | solution.py:201
  198.1 0.6 fusion.265
  199.1 0.4 convolution_add_fusion.28
  200.7 0.4 convolution_add_fusion.30
  201.5 0.4 convolution_add_fusion.31
  202.3 0.4 convolution_add_fusion.32
  202.9 0.6 fusion.271
  204.0 0.6 convolution_multiply_fusion.8
  204.6 0.6 convolution_multiply_fusion.9
  205.2 0.4 fusion.273
  205.7 1.2 convolution_add_fusion.33
  207.2 0.6 fusion.265
  208.2 0.4 convolution_add_fusion.28
  209.8 0.4 convolution_add_fusion.30
  210.6 0.4 convolution_add_fusion.31
  211.4 0.4 convolution_add_fusion.32
  212.1 0.6 fusion.271
  213.1 0.6 convolution_multiply_fusion.8
  213.7 0.6 convolution_multiply_fusion.9
  214.3 0.4 fusion.273
  214.9 1.2 convolution_add_fusion.33
  216.9 1.0 fusion.72
  (121 shorter events, 17.6 us)
Async XLA Ops:
  6.5 31.4 %copy-start = (f32[128]{0:T(128)S(1)}, f32[128]{0:T(128)}, u32[]{:S(2)}) copy-start(f32[128]{0:T(128)} %param.29) | copy-start | bytes 1540
  6.5 9.8 %copy-start.3 = (bf16[128,1024]{1,0:T(8,128)(2,1)S(1)}, bf16[128,1024]{1,0:T(8,128)(2,1)}, u32[]{:S(2)}) copy-start(bf16[128,1024]{1,0:T(8,128)(2,1)} %param.20) | copy-start | bytes 786436
  6.5 103.4 %all-gather.5.cloned.1.call-start = ((), (), s32[]{:S(2)}) async-start(), calls=%async_computation | async-start | bytes 4718592 | tf_op jit(solution)/shard_map/all_gather | solution.py:22
  8.8 5.6 %collective-permute-start = (bf16[3,2048]{1,0:T(4,128)(2,1)S(1)}, bf16[3,2048]{1,0:T(4,128)(2,1)S(1)}, u32[]{:S(2)}, u32[]{:S(2)}) collective-permute-start(bf16[3,2048]{1,0:T(4,128)(2,1)S(1)} %pad_maximum_fusion), channel_id=1, source_target_pairs={{0,2},{2,4},{4,6},{6,8},{8,10},{10,12},{12,14},{1,3},{3,5},{5,7},{... | collective-permute-start | bytes 36872 | tf_op jit(solution)/shard_map/ppermute | solution.py:17
  17.0 21.0 %copy-start.5 = (bf16[4,512]{1,0:T(4,128)(2,1)S(1)}, bf16[4,512]{1,0:T(4,128)(2,1)}, u32[]{:S(2)}) copy-start(bf16[4,512]{1,0:T(4,128)(2,1)} %param.24) | copy-start | bytes 12292
  36.3 0.8 copy-start.2
  36.4 1.1 copy-start.1
  37.2 146.6 %all-gather.7.cloned.1.call-start = ((), (), s32[]{:S(2)}) async-start(), calls=%async_computation.1 | async-start | bytes 4718592 | tf_op jit(solution)/shard_map/all_gather | solution.py:22
  197.8 19.1 %copy-start.4 = (bf16[128,1024]{1,0:T(8,128)(2,1)S(1)}, bf16[128,1024]{1,0:T(8,128)(2,1)}, u32[]{:S(2)}) copy-start(bf16[128,1024]{1,0:T(8,128)(2,1)} %param.21) | copy-start | bytes 786436
Sparse Core Ops, SparseCore 0:
  37.3 72.5 all-gather.4
  112.1 71.6 all-gather.6
where the time goes:
time: 225 us
  waiting for transfers between devices  146 us (65%)
  matrix products  47 us (21%)
  between operations  13.8 us (6%)
  other arithmetic  9.29 us (4%)
  local copies, waits for them, and re-layouts  6.4 us (3%)
    all_gather x2, waiting for transfers between devices, carried_in(): gathered = jax.tree.map(lambda a: lax.all_gather(a, axis), part)  145 us
    dot_general x73, matrix products, mixing_weight(): return jnp.einsum(form, left, right, precision=HIGH)  47 us
  transfers between devices with their start and end apart: 3, of which 3 were waited for; matrix products, arithmetic and copies ran while one was open for 2% of the time, Pallas kernels for 0%

commit v1 on v0

v1 whole, which is shorter than its diff:
```python
import functools

import jax
import jax.numpy as jnp
from jax import lax
from jax.experimental import pallas as pl
from jax.experimental.pallas import tpu as pltpu
from jax.sharding import PartitionSpec as P

MESH = pl.DeviceIdType.MESH
HIGH = lax.Precision.HIGHEST
RIM = 16
BF = jnp.bfloat16
F32 = jnp.float32


def mm(a, b):
    return jnp.dot(a.astype(BF), b.astype(BF), preferred_element_type=F32)


def mm_nt(a, b):
    return lax.dot_general(a.astype(BF), b.astype(BF), (((1,), (1,)), ((), ())), preferred_element_type=F32)


def mm_tn(a, b):
    return jnp.dot(a.astype(BF).T, b.astype(BF), preferred_element_type=F32)


def conv_silu(full, weights, count):
    taps = weights.shape[0]
    total = weights[0:1].astype(F32) * full(0)
    for i in range(1, taps):
        total = total + weights[i : i + 1].astype(F32) * full(i)
    return (total * jax.nn.sigmoid(total)).astype(BF)


def block_maps(qs, ks, vs, beta_logit, decay_in, a_log, dt_bias, repeat):
    rows, size = qs[0].shape
    heads = len(vs)
    kheads = len(ks)
    row = lax.broadcasted_iota(jnp.int32, (rows, rows), 0)
    col = lax.broadcasted_iota(jnp.int32, (rows, rows), 1)
    lane = lax.broadcasted_iota(jnp.int32, (rows, 128), 1)
    later = row >= col
    beta = jax.nn.sigmoid(beta_logit)
    x = decay_in + dt_bias
    soft = jnp.maximum(x, 0.0) + jnp.log1p(jnp.exp(-jnp.abs(x)))
    decay = -jnp.exp(a_log) * soft
    cum = jnp.dot(later.astype(F32), decay, precision=HIGH, preferred_element_type=F32)
    growth = jnp.exp(cum)
    tail = jnp.exp(cum[rows - 1 : rows] - cum)

    def norm(block):
        block = block.astype(F32)
        return 1.0 / jnp.sqrt(jnp.sum(block * block, axis=-1, keepdims=True) + 1e-06)

    qn = [norm(q) * size ** (-0.5) for q in qs]
    kn = [norm(k) for k in ks]
    stats = jnp.zeros((rows, 128), F32)
    for h in range(heads):
        stats = jnp.where(lane == h, cum[:, h : h + 1], stats)
        stats = jnp.where(lane == heads + h, beta[:, h : h + 1], stats)
    for j in range(kheads):
        stats = jnp.where(lane == 2 * heads + j, kn[j], stats)
    stats = stats.T
    inner = [mm_nt(k, k) for k in ks]
    cross = [mm_nt(q, k) for q, k in zip(qs, ks)]
    lower, score = [], []
    for h in range(heads):
        j = h // repeat
        cum_row, kn_row = stats[h : h + 1], stats[2 * heads + j : 2 * heads + j + 1]
        ratio = jnp.where(later, jnp.exp(jnp.minimum(cum[:, h : h + 1] - cum_row, 0.0)), 0.0) * kn_row
        lower.append(jnp.where(row > col, ratio * inner[j] * (beta[:, h : h + 1] * kn[j]), 0.0))
        score.append(ratio * cross[j] * qn[j])
    eye = (row == col).astype(F32)
    inv = [eye - jnp.where(row // 2 == col // 2, m, 0.0) for m in lower]
    step = 2
    while step < rows:
        mask = (row // (2 * step) == col // (2 * step)) & (row // step != col // step)
        edge = [mm(jnp.where(mask, lower[h], 0.0), inv[h]) for h in range(heads)]
        inv = [inv[h] - mm(inv[h], edge[h]) for h in range(heads)]
        step *= 2
    update, folded = [], []
    for h in range(heads):
        j = h // repeat
        beta_row = stats[heads + h : heads + h + 1]
        gain_row = beta_row * jnp.exp(stats[h : h + 1]) * stats[2 * heads + j : 2 * heads + j + 1]
        update.append(mm(inv[h] * beta_row, vs[h]).astype(BF))
        folded.append(mm(inv[h] * gain_row, ks[j]).astype(BF))
    result = []
    for h in range(heads):
        j = h // repeat
        key_tail = (ks[j].astype(F32) * (kn[j] * tail[:, h : h + 1])).astype(BF)
        both = jnp.concatenate([folded[h], update[h]], axis=1)
        ends = mm_tn(key_tail, both)
        inside = mm(score[h], both)
        reach = qs[j].astype(F32) * (qn[j] * growth[:, h : h + 1]) - inside[:, :size]
        last = jnp.broadcast_to(growth[rows - 1 : rows, h : h + 1], (1, 128))
        result.append((-ends[:, :size], last, ends[:, size:], reach, inside[:, size:]))
    return result


def halo_kernel(axis, n, q_ref, k_ref, v_ref, hq_ref, hk_ref, hv_ref, send_sem, recv_sem):
    me = lax.axis_index(axis)
    rows = q_ref.shape[0]
    first, last = me == 0, me == n - 1
    barrier = pltpu.get_barrier_semaphore()

    @pl.when(jnp.logical_not(first))
    def _():
        pl.semaphore_signal(barrier, inc=1, device_id={axis: me - 1}, device_id_type=MESH)

    @pl.when(jnp.logical_not(last))
    def _():
        pl.semaphore_signal(barrier, inc=1, device_id={axis: me + 1}, device_id_type=MESH)

    pl.semaphore_wait(barrier, jnp.where(first, 0, 1) + jnp.where(last, 0, 1))

    def copies(to):
        return [
            pltpu.make_async_remote_copy(
                src_ref=src.at[pl.ds(rows - RIM, RIM), :],
                dst_ref=dst,
                send_sem=send_sem.at[i],
                recv_sem=recv_sem.at[i],
                device_id={axis: to},
                device_id_type=MESH,
            )
            for i, (src, dst) in enumerate(((q_ref, hq_ref), (k_ref, hk_ref), (v_ref, hv_ref)))
        ]

    @pl.when(jnp.logical_not(last))
    def _():
        for copy in copies(me + 1):
            copy.start()

    @pl.when(first)
    def _():
        for ref in (hq_ref, hk_ref, hv_ref):
            ref[...] = jnp.zeros_like(ref)

    @pl.when(jnp.logical_not(first))
    def _():
        for copy in copies(me - 1):
            copy.wait_recv()

    @pl.when(jnp.logical_not(last))
    def _():
        for copy in copies(me + 1):
            copy.wait_send()


def local_kernel(
    q_ref, k_ref, v_ref, hq_ref, hk_ref, hv_ref, bl_ref, di_ref, wq_ref, wk_ref, wv_ref, al_ref, dt_ref,
    m_ref, g_ref, b_ref, p_ref, o_ref, fq_ref, fk_ref, fv_ref,
):
    rows = q_ref.shape[0]
    size = m_ref.shape[-1]
    taps = wq_ref.shape[0]
    blocks = []
    for x_ref, h_ref, w_ref, f_ref in (
        (q_ref, hq_ref, wq_ref, fq_ref), (k_ref, hk_ref, wk_ref, fk_ref), (v_ref, hv_ref, wv_ref, fv_ref)
    ):
        f_ref[pl.ds(0, RIM), :] = h_ref[...].astype(F32)
        f_ref[pl.ds(RIM, rows), :] = x_ref[...].astype(F32)
        parts = []
        for c in range(x_ref.shape[1] // size):
            lanes = pl.ds(c * size, size)
            parts.append(conv_silu(lambda i: f_ref[pl.ds(RIM - taps + 1 + i, rows), lanes], w_ref[:, lanes], rows))
        blocks.append(parts)
    qs, ks, vs = blocks
    maps = block_maps(qs, ks, vs, bl_ref[...], di_ref[...], al_ref[...], dt_ref[...], len(vs) // len(ks))
    for h, (move, last, base, reach, inside) in enumerate(maps):
        m_ref[h] = move.astype(BF)
        g_ref[pl.ds(h, 1), :] = last
        b_ref[h] = base
        p_ref[h] = reach.astype(BF)
        o_ref[h] = inside


def chain_kernel(
    axis, n, m_ref, g_ref, b_ref, p_ref, o_ref, z_ref, gain_ref, out_ref, held, sent, send_sem, recv_sem
):
    me = lax.axis_index(axis)
    heads, _, size = m_ref.shape
    first, last = me == 0, me == n - 1
    barrier = pltpu.get_barrier_semaphore()

    @pl.when(jnp.logical_not(first))
    def _():
        pl.semaphore_signal(barrier, inc=1, device_id={axis: me - 1}, device_id_type=MESH)

    @pl.when(jnp.logical_not(last))
    def _():
        pl.semaphore_signal(barrier, inc=1, device_id={axis: me + 1}, device_id_type=MESH)

    pl.semaphore_wait(barrier, jnp.where(first, 0, 1) + jnp.where(last, 0, 1))

    @pl.when(first)
    def _():
        held[...] = jnp.zeros_like(held)

    def hop(h, to):
        return pltpu.make_async_remote_copy(
            src_ref=sent.at[h],
            dst_ref=held.at[h],
            send_sem=send_sem.at[h],
            recv_sem=recv_sem.at[h],
            device_id={axis: to},
            device_id_type=MESH,
        )

    for h in range(heads):

        @pl.when(jnp.logical_not(first))
        def _():
            hop(h, me - 1).wait_recv()

        @pl.when(jnp.logical_not(last))
        def _():
            state = held[h]
            fresh = b_ref[h] + g_ref[pl.ds(h, 1), :] * state.astype(F32)
            fresh = fresh + jnp.dot(m_ref[h], state, preferred_element_type=F32)
            sent[h] = fresh.astype(sent.dtype)
            hop(h, me + 1).start()

    gain = gain_ref[...]
    for h in range(heads):
        lanes = pl.ds(h * size, size)
        mixed = o_ref[h] + jnp.dot(p_ref[h], held[h], preferred_element_type=F32)
        scale = lax.rsqrt(jnp.mean(mixed * mixed, axis=-1, keepdims=True) + 1e-06)
        gate = z_ref[:, lanes].astype(F32)
        out_ref[:, lanes] = (mixed * scale * gain * (gate * jax.nn.sigmoid(gate))).astype(out_ref.dtype)

    @pl.when(jnp.logical_not(last))
    def _():
        for h in range(heads):
            hop(h, me + 1).wait_send()


def vmem(count):
    return [pl.BlockSpec(memory_space=pltpu.VMEM)] * count


def per_device(n, q_raw, k_raw, v_raw, gate_z, beta_logit, decay_in, conv_q, conv_k, conv_v, a_log, dt_bias, norm_gain):
    size = norm_gain.shape[0]
    rows, width = q_raw.shape
    vwidth = v_raw.shape[1]
    heads = vwidth // size
    halos = pl.pallas_call(
        functools.partial(halo_kernel, "context", n),
        out_shape=[jax.ShapeDtypeStruct((RIM, w), BF) for w in (width, width, vwidth)],
        in_specs=[pl.BlockSpec(memory_space=pl.ANY)] * 3,
        out_specs=vmem(3),
        scratch_shapes=[pltpu.SemaphoreType.DMA((3,)), pltpu.SemaphoreType.DMA((3,))],
        compiler_params=pltpu.CompilerParams(collective_id=0, has_side_effects=True),
        name="halo",
    )(q_raw, k_raw, v_raw)
    square = (heads, size, size)
    tall = (heads, rows, size)
    maps = pl.pallas_call(
        local_kernel,
        out_shape=[
            jax.ShapeDtypeStruct(square, BF),
            jax.ShapeDtypeStruct((heads, 128), F32),
            jax.ShapeDtypeStruct(square, F32),
            jax.ShapeDtypeStruct(tall, BF),
            jax.ShapeDtypeStruct(tall, F32),
        ],
        in_specs=vmem(13),
        out_specs=vmem(5),
        scratch_shapes=[pltpu.VMEM((rows + RIM, w), F32) for w in (width, width, vwidth)],
        compiler_params=pltpu.CompilerParams(vmem_limit_bytes=48 << 20),
        name="local",
    )(q_raw, k_raw, v_raw, *halos, beta_logit, decay_in, conv_q, conv_k, conv_v, a_log[None], dt_bias[None])
    return pl.pallas_call(
        functools.partial(chain_kernel, "context", n),
        out_shape=jax.ShapeDtypeStruct((rows, vwidth), BF),
        in_specs=vmem(7),
        out_specs=pl.BlockSpec(memory_space=pltpu.VMEM),
        scratch_shapes=[
            pltpu.VMEM(square, BF),
            pltpu.VMEM(square, BF),
            pltpu.SemaphoreType.DMA((heads,)),
            pltpu.SemaphoreType.DMA((heads,)),
        ],
        compiler_params=pltpu.CompilerParams(collective_id=1, has_side_effects=True),
        name="chain",
    )(*maps, gate_z, norm_gain[None])


def solution(mesh):
    rows = P(("groups", "context"), "tensor")
    return jax.shard_map(
        functools.partial(per_device, mesh.shape["context"]),
        mesh=mesh,
        in_specs=(rows,) * 6 + (P(None, "tensor"),) * 3 + (P("tensor"),) * 2 + (P(),),
        out_specs=rows,
        check_vma=False,
    )
```

time: 225 us -> 47.1 us (0.21)
  waiting for transfers between devices: 146 us -> 0 us
  matrix products: 47 us -> 0 us
  Pallas kernels: 0 us -> 36.9 us
  between operations: 13.8 us -> 0.13 us
  other arithmetic: 9.29 us -> 0 us
  local copies, waits for them, and re-layouts: 6.4 us -> 9.58 us
    all_gather x2 -> x0, waiting for transfers between devices: 145 us -> none  [carried_in(): gathered = jax.tree.map(lambda a: lax.all_gather(a, axis), part)]
    dot_general x73 -> x0, matrix products: 47 us -> none  [mixing_weight(): return jnp.einsum(form, left, right, precision=HIGH)]
    pallas_call x0 -> x3, Pallas kernels: none -> 36.9 us  [the longest x1 27.7 us: per_device(): pl.pallas_call(functools.partial(chain_kernel, 'context', n), out_shape=j...]
    unnamed x16 -> x39, local copies, waits for them, and re-layouts: 1.15 us -> 9.58 us
    slice x13 -> x0, local copies, waits for them, and re-layouts: 3.67 us -> none  [the longest x1 0.79 us: per_device(): v_raw[rows - taps + 1:]]
    mul x9 -> x0, other arithmetic: 3.11 us -> none  [the longest x3 1.72 us: causal_conv(): weights[place].astype(jnp.float32)[None, :] * full[place:place + count]]
  transfers between devices with their start and end apart: 3 -> 0, of which waited for: 3 -> 0; matrix products, arithmetic and copies ran while one was open for 2% -> 0% of each run, Pallas kernels for 0% -> 0%
where the time goes in v1:
time: 47.1 us; the launch traced here: 46.6 us
  Pallas kernels  36.9 us (78%)
  local copies, waits for them, and re-layouts  9.58 us (20%)
    pallas_call x1, Pallas kernels, per_device(): pl.pallas_call(functools.partial(chain_kernel, 'context', n), out_shape=j...  27.7 us
    unnamed x39, local copies, waits for them, and re-layouts  9.58 us
    pallas_call x1, Pallas kernels, per_device(): pl.pallas_call(functools.partial(halo_kernel, 'context', n), out_shape=[j...  5.2 us
    pallas_call x1, Pallas kernels, per_device(): pl.pallas_call(local_kernel, out_shape=[jax.ShapeDtypeStruct(square, BF),...  4.07 us

profile of v1, /device:TPU:26, one launch (start us, length us, event | category | flops | bytes accessed | tf_op | source)
XLA Modules:
  0.0 46.6 jit_solution(8294286986964069750)
XLA Ops:
  0.0 0.0 copy-start.16
  0.0 0.7 %copy-done.16 = f32[128,8]{0,1:T(8,128)S(1)} copy-done((f32[128,8]{0,1:T(8,128)S(1)}, f32[128,8]{0,1:T(8,128)}, u32[]{:S(2)}) %copy-start.16) | copy-done | bytes 4120
  0.7 0.0 copy-start.17
  0.7 0.1 copy.13.bl_ref
  0.8 0.6 %copy-done.17 = f32[128,8]{0,1:T(8,128)S(1)} copy-done((f32[128,8]{0,1:T(8,128)S(1)}, f32[128,8]{0,1:T(8,128)}, u32[]{:S(2)}) %copy-start.17) | copy-done | bytes 4120
  1.4 0.0 copy-start.10
  1.4 0.0 copy-start.12
  1.4 0.1 copy.14.di_ref
  1.5 0.0 copy-start
  1.5 0.0 copy-start.3
  1.5 0.0 copy-start.4
  1.5 5.2 %halo.1 = (bf16[16,512]{1,0:T(8,128)(2,1)}, bf16[16,512]{1,0:T(8,128)(2,1)}, bf16[16,1024]{1,0:T(8,128)(2,1)}) custom-call(bf16[128,512]{1,0:T(8,128)(2,1)} %q_ref.3, bf16[128,512]{1,0:T(8,128)(2,1)} %k_ref.3, bf16[128,1024]{1,0:T(8,128)(2,1)} %v_ref.3), custom_call_target="tpu_custom_call" | custom-call | tf_op jit(solution)/shard_map/halo/pallas_call | solution.py:250
  6.7 0.0 copy-start.11
  6.7 0.0 copy-start.14
  6.7 0.0 copy-start.15
  6.8 0.0 copy-done.10
  6.8 0.0 copy-done.12
  6.8 0.0 copy-done
  6.8 0.0 copy-done.3
  6.8 0.0 copy-done.4
  6.8 0.6 %copy-done.11 = bf16[4,512]{1,0:T(4,128)(2,1)S(1)} copy-done((bf16[4,512]{1,0:T(4,128)(2,1)S(1)}, bf16[4,512]{1,0:T(4,128)(2,1)}, u32[]{:S(2)}) %copy-start.11) | copy-done | bytes 4120
  7.4 0.0 copy-done.14
  7.4 0.0 copy-done.15
  7.4 0.0 copy-start.7
  7.4 0.8 %copy-done.7 = bf16[16,1024]{1,0:T(8,128)(2,1)S(1)} copy-done((bf16[16,1024]{1,0:T(8,128)(2,1)S(1)}, bf16[16,1024]{1,0:T(8,128)(2,1)}, u32[]{:S(2)}) %copy-start.7) | copy-done | bytes 32792
  8.2 0.0 copy-start.8
  8.2 0.7 %copy-done.8 = bf16[16,512]{1,0:T(8,128)(2,1)S(1)} copy-done((bf16[16,512]{1,0:T(8,128)(2,1)S(1)}, bf16[16,512]{1,0:T(8,128)(2,1)}, u32[]{:S(2)}) %copy-start.8) | copy-done | bytes 16408
  8.9 0.0 copy-start.9
  8.9 0.7 %copy-done.9 = bf16[16,512]{1,0:T(8,128)(2,1)S(1)} copy-done((bf16[16,512]{1,0:T(8,128)(2,1)S(1)}, bf16[16,512]{1,0:T(8,128)(2,1)}, u32[]{:S(2)}) %copy-start.9) | copy-done | bytes 16408
  9.6 4.1 %local.1 = (bf16[8,128,128]{2,1,0:T(8,128)(2,1)S(1)}, f32[8,128]{1,0:T(8,128)S(1)}, f32[8,128,128]{2,1,0:T(8,128)S(1)}, bf16[8,128,128]{2,1,0:T(8,128)(2,1)S(1)}, f32[8,128,128]{2,1,0:T(8,128)S(1)}) custom-call(bf16[128,512]{1,0:T(8,128)(2,1)S(1)} %copy-done.3, bf16[128,512]{1,0:T(8,128)(2,1)S(1)} %copy-done.4, bf16[128,1024]{1,0:T(8,128)(2,1)S(1)} %copy-done, ...), custom_call_target="tpu_custom_call" | custom-call | tf_op jit(solution)/shard_map/local/pallas_call | solution.py:261
  13.7 0.0 copy-start.1
  13.7 0.8 %copy-done.1 = f32[8,128,128]{2,1,0:T(8,128)} copy-done((f32[8,128,128]{2,1,0:T(8,128)}, f32[8,128,128]{2,1,0:T(8,128)S(1)}, u32[]{:S(2)}) %copy-start.1) | copy-done | bytes 524312
  14.5 0.0 copy-start.2
  14.5 0.8 %copy-done.2 = f32[8,128,128]{2,1,0:T(8,128)} copy-done((f32[8,128,128]{2,1,0:T(8,128)}, f32[8,128,128]{2,1,0:T(8,128)S(1)}, u32[]{:S(2)}) %copy-start.2) | copy-done | bytes 524312
  15.3 0.0 copy-start.5
  15.3 0.7 %copy-done.5 = bf16[8,128,128]{2,1,0:T(8,128)(2,1)} copy-done((bf16[8,128,128]{2,1,0:T(8,128)(2,1)}, bf16[8,128,128]{2,1,0:T(8,128)(2,1)S(1)}, u32[]{:S(2)}) %copy-start.5) | copy-done | bytes 262168
  16.0 0.0 copy-start.6
  16.0 0.7 %copy-done.6 = bf16[8,128,128]{2,1,0:T(8,128)(2,1)} copy-done((bf16[8,128,128]{2,1,0:T(8,128)(2,1)}, bf16[8,128,128]{2,1,0:T(8,128)(2,1)S(1)}, u32[]{:S(2)}) %copy-start.6) | copy-done | bytes 262168
  16.7 0.0 copy-start.13
  16.7 0.6 %copy-done.13 = f32[8,128]{1,0:T(8,128)} copy-done((f32[8,128]{1,0:T(8,128)}, f32[8,128]{1,0:T(8,128)S(1)}, u32[]{:S(2)}) %copy-start.13) | copy-done | bytes 4120
  17.3 27.7 %chain.1 = bf16[128,1024]{1,0:T(8,128)(2,1)} custom-call(bf16[8,128,128]{2,1,0:T(8,128)(2,1)} %copy-done.5, f32[8,128]{1,0:T(8,128)} %copy-done.13, f32[8,128,128]{2,1,0:T(8,128)} %copy-done.1, bf16[8,128,128]{2,1,0:T(8,128)(2,1)} %copy-done.6, f32[8,128,128]{2,1,0:T(8,128)} %copy-done.2, bf16[128,1024]{1,0:T(8,128)(2,1)} %z_ref.1, f32[1,128]{1,0:T(1,128)} %bitcast.5), custom_call_target="tpu_custom_call" | custom-call | tf_op jit(solution)/shard_map/chain/pallas_call | solution.py:276
  45.0 1.7 %copy.16 = bf16[128,1024]{1,0:T(8,128)(2,1)} copy(bf16[128,1024]{1,0:T(8,128)(2,1)} %chain.1) | data formatting | bytes 524288
Async XLA Ops:
  0.0 0.7 %copy-start.16 = (f32[128,8]{0,1:T(8,128)S(1)}, f32[128,8]{0,1:T(8,128)}, u32[]{:S(2)}) copy-start(f32[128,8]{0,1:T(8,128)} %param.16) | copy-start | bytes 12292
  0.7 0.7 %copy-start.17 = (f32[128,8]{0,1:T(8,128)S(1)}, f32[128,8]{0,1:T(8,128)}, u32[]{:S(2)}) copy-start(f32[128,8]{0,1:T(8,128)} %param.17) | copy-start | bytes 12292
  1.4 5.4 %copy-start.10 = (bf16[4,1024]{1,0:T(4,128)(2,1)S(1)}, bf16[4,1024]{1,0:T(4,128)(2,1)}, u32[]{:S(2)}) copy-start(bf16[4,1024]{1,0:T(4,128)(2,1)} %wv_ref.1) | copy-start | bytes 24580
  1.4 5.4 %copy-start.12 = (bf16[4,512]{1,0:T(4,128)(2,1)S(1)}, bf16[4,512]{1,0:T(4,128)(2,1)}, u32[]{:S(2)}) copy-start(bf16[4,512]{1,0:T(4,128)(2,1)} %wk_ref.1) | copy-start | bytes 12292
  1.5 5.3 %copy-start = (bf16[128,1024]{1,0:T(8,128)(2,1)S(1)}, bf16[128,1024]{1,0:T(8,128)(2,1)}, u32[]{:S(2)}) copy-start(bf16[128,1024]{1,0:T(8,128)(2,1)} %v_ref.3) | copy-start | bytes 786436
  1.5 5.3 %copy-start.3 = (bf16[128,512]{1,0:T(8,128)(2,1)S(1)}, bf16[128,512]{1,0:T(8,128)(2,1)}, u32[]{:S(2)}) copy-start(bf16[128,512]{1,0:T(8,128)(2,1)} %q_ref.3) | copy-start | bytes 393220
  1.5 5.3 %copy-start.4 = (bf16[128,512]{1,0:T(8,128)(2,1)S(1)}, bf16[128,512]{1,0:T(8,128)(2,1)}, u32[]{:S(2)}) copy-start(bf16[128,512]{1,0:T(8,128)(2,1)} %k_ref.3) | copy-start | bytes 393220
  6.7 0.7 %copy-start.11 = (bf16[4,512]{1,0:T(4,128)(2,1)S(1)}, bf16[4,512]{1,0:T(4,128)(2,1)}, u32[]{:S(2)}) copy-start(bf16[4,512]{1,0:T(4,128)(2,1)} %wq_ref.1) | copy-start | bytes 12292
  6.7 0.7 %copy-start.14 = (f32[8]{0:T(128)S(1)}, f32[8]{0:T(128)}, u32[]{:S(2)}) copy-start(f32[8]{0:T(128)} %param.21) | copy-start | bytes 100
  6.7 0.7 %copy-start.15 = (f32[8]{0:T(128)S(1)}, f32[8]{0:T(128)}, u32[]{:S(2)}) copy-start(f32[8]{0:T(128)} %param.22) | copy-start | bytes 100
  7.4 0.8 %copy-start.7 = (bf16[16,1024]{1,0:T(8,128)(2,1)S(1)}, bf16[16,1024]{1,0:T(8,128)(2,1)}, u32[]{:S(2)}) copy-start(bf16[16,1024]{1,0:T(8,128)(2,1)} %get-tuple-element.15.hv_ref) | copy-start | bytes 98308
  8.2 0.7 %copy-start.8 = (bf16[16,512]{1,0:T(8,128)(2,1)S(1)}, bf16[16,512]{1,0:T(8,128)(2,1)}, u32[]{:S(2)}) copy-start(bf16[16,512]{1,0:T(8,128)(2,1)} %get-tuple-element.13.hq_ref) | copy-start | bytes 49156
  8.9 0.7 %copy-start.9 = (bf16[16,512]{1,0:T(8,128)(2,1)S(1)}, bf16[16,512]{1,0:T(8,128)(2,1)}, u32[]{:S(2)}) copy-start(bf16[16,512]{1,0:T(8,128)(2,1)} %get-tuple-element.14.hk_ref) | copy-start | bytes 49156
  13.7 0.8 %copy-start.1 = (f32[8,128,128]{2,1,0:T(8,128)}, f32[8,128,128]{2,1,0:T(8,128)S(1)}, u32[]{:S(2)}) copy-start(f32[8,128,128]{2,1,0:T(8,128)S(1)} %get-tuple-element.18.b_ref) | copy-start | bytes 1572868
  14.5 0.8 %copy-start.2 = (f32[8,128,128]{2,1,0:T(8,128)}, f32[8,128,128]{2,1,0:T(8,128)S(1)}, u32[]{:S(2)}) copy-start(f32[8,128,128]{2,1,0:T(8,128)S(1)} %get-tuple-element.20.o_ref) | copy-start | bytes 1572868
  15.3 0.7 %copy-start.5 = (bf16[8,128,128]{2,1,0:T(8,128)(2,1)}, bf16[8,128,128]{2,1,0:T(8,128)(2,1)S(1)}, u32[]{:S(2)}) copy-start(bf16[8,128,128]{2,1,0:T(8,128)(2,1)S(1)} %get-tuple-element.16.m_ref) | copy-start | bytes 786436
  16.0 0.7 %copy-start.6 = (bf16[8,128,128]{2,1,0:T(8,128)(2,1)}, bf16[8,128,128]{2,1,0:T(8,128)(2,1)S(1)}, u32[]{:S(2)}) copy-start(bf16[8,128,128]{2,1,0:T(8,128)(2,1)S(1)} %get-tuple-element.19.p_ref) | copy-start | bytes 786436
  16.7 0.6 %copy-start.13 = (f32[8,128]{1,0:T(8,128)}, f32[8,128]{1,0:T(8,128)S(1)}, u32[]{:S(2)}) copy-start(f32[8,128]{1,0:T(8,128)S(1)} %get-tuple-element.17.g_ref) | copy-start | bytes 12292

commit v2 on v1

v2 whole, which is shorter than its diff:
```python
import functools
import math

import jax
import jax.numpy as jnp
from jax import lax
from jax.experimental import pallas as pl
from jax.experimental.pallas import tpu as pltpu
from jax.sharding import PartitionSpec as P

MESH = pl.DeviceIdType.MESH
HIGH = lax.Precision.HIGHEST
RIM = 16
BF = jnp.bfloat16
F32 = jnp.float32


def mm(a, b):
    return jnp.dot(a.astype(BF), b.astype(BF), preferred_element_type=F32)


def mm_nt(a, b):
    return lax.dot_general(a.astype(BF), b.astype(BF), (((1,), (1,)), ((), ())), preferred_element_type=F32)


def mm_tn(a, b):
    return jnp.dot(a.astype(BF).T, b.astype(BF), preferred_element_type=F32)


def conv_silu(full, weights, count):
    taps = weights.shape[0]
    total = weights[0:1].astype(F32) * full(0)
    for i in range(1, taps):
        total = total + weights[i : i + 1].astype(F32) * full(i)
    return (total * jax.nn.sigmoid(total)).astype(BF)


def block_maps(qs, ks, vs, beta_rows, decay_rows, repeat):
    rows, size = qs[0].shape
    units = len(vs)
    row = lax.broadcasted_iota(jnp.int32, (rows, rows), 0)
    col = lax.broadcasted_iota(jnp.int32, (rows, rows), 1)
    later = row >= col
    cum_rows = jnp.dot(decay_rows, (row <= col).astype(F32), precision=HIGH, preferred_element_type=F32)
    pad = jnp.zeros((rows - 2 * units, rows), F32)
    columns = jnp.concatenate([cum_rows, beta_rows, pad], axis=0).T
    cum, beta = columns[:, :units], columns[:, units : 2 * units]
    growth = jnp.exp(cum)
    tail = jnp.exp(cum[rows - 1 : rows] - cum)

    def norm(block):
        block = block.astype(F32)
        return 1.0 / jnp.sqrt(jnp.sum(block * block, axis=-1, keepdims=True) + 1e-06)

    qn = [norm(q) * size ** (-0.5) for q in qs]
    kn = [norm(k) for k in ks]
    kn_rows = jnp.zeros((rows, rows), F32)
    for j, column in enumerate(kn):
        kn_rows = jnp.where(col == j, column, kn_rows)
    kn_rows = kn_rows.T
    inner = [mm_nt(k, k) for k in ks]
    cross = [mm_nt(q, k) for q, k in zip(qs, ks)]
    lower, score = [], []
    for h in range(units):
        j = h // repeat
        ratio = jnp.exp(jnp.minimum(cum[:, h : h + 1] - cum_rows[h : h + 1], 0.0))
        ratio = jnp.where(later, ratio, 0.0) * kn_rows[j : j + 1]
        lower.append(jnp.where(row > col, ratio * inner[j] * (beta[:, h : h + 1] * kn[j]), 0.0))
        score.append((ratio * cross[j] * qn[j]).astype(BF))
    eye = (row == col).astype(F32)
    inv = [eye - jnp.where(row // 2 == col // 2, m, 0.0) for m in lower]
    step = 2
    while step < rows:
        mask = (row // (2 * step) == col // (2 * step)) & (row // step != col // step)
        edge = [mm(jnp.where(mask, lower[h], 0.0), inv[h]) for h in range(units)]
        inv = [inv[h] - mm(inv[h], edge[h]) for h in range(units)]
        step *= 2
    update, folded = [], []
    for h in range(units):
        j = h // repeat
        beta_row = beta_rows[h : h + 1]
        gain_row = beta_row * jnp.exp(cum_rows[h : h + 1]) * kn_rows[j : j + 1]
        update.append(mm(inv[h] * beta_row, vs[h]).astype(BF))
        folded.append(mm(inv[h] * gain_row, ks[j]).astype(BF))
    result = []
    for h in range(units):
        j = h // repeat
        key_tail = (ks[j].astype(F32) * (kn[j] * tail[:, h : h + 1])).astype(BF)
        both = jnp.concatenate([folded[h], update[h]], axis=1)
        ends = mm_tn(key_tail, both)
        inside = mm(score[h], both)
        reach = qs[j].astype(F32) * (qn[j] * growth[:, h : h + 1]) - inside[:, :size]
        last = jnp.broadcast_to(growth[rows - 1 : rows, h : h + 1], (1, size))
        result.append((-ends[:, :size], last, ends[:, size:], reach, inside[:, size:]))
    return result


def mixer_kernel(
    axis, n, team, size,
    q_ref, k_ref, v_ref, bl_ref, di_ref, wq_ref, wk_ref, wv_ref, al_ref, dt_ref, gain_ref,
    out_ref,
    q_rows, k_rows, v_rows, logits, inputs, wq, wk, wv, al, dt, gain,
    fq, fk, fv, m_s, g_s, b_s, p_s, o_s, held, sent, back,
    local_sem, send_sem, recv_sem, rim_send, rim_recv, hop_send, hop_recv, back_send, back_recv,
):
    me = lax.axis_index(axis)
    place, turn = lax.rem(me, team), me // team
    base = turn * team
    rows = q_ref.shape[0]
    taps = wq_ref.shape[0]
    kw, vw = wq_ref.shape[1] // team, wv_ref.shape[1] // team
    kpm, hpm = kw // size, vw // size
    repeat = hpm // kpm
    units = team * hpm
    first, last = turn == 0, turn == n // team - 1
    tail_place = place == team - 1
    streams = ((q_ref, q_rows, kw), (k_ref, k_rows, kw), (v_ref, v_rows, vw))
    whole = ((bl_ref, logits), (di_ref, inputs))

    def lanes_of(who, width):
        return pl.ds(pl.multiple_of(who * width, width), width)

    def rows_of(who):
        return pl.ds(pl.multiple_of(RIM + who * rows, RIM), rows)

    staying = []
    for i, (src, dst, width) in enumerate(streams):
        staying.append((src.at[:, lanes_of(place, width)], dst.at[rows_of(place), :]))
    for src, dst in whole:
        staying.append((src, dst.at[place]))
    for src, dst, width in ((wq_ref, wq, kw), (wk_ref, wk, kw), (wv_ref, wv, vw)):
        staying.append((src.at[:, lanes_of(place, width)], dst))
    staying += [(al_ref, al), (dt_ref, dt), (gain_ref, gain)]
    staying = [pltpu.make_async_copy(a, b, local_sem.at[i]) for i, (a, b) in enumerate(staying)]
    for copy in staying:
        copy.start()

    barrier = pltpu.get_barrier_semaphore()

    def greet(who):
        pl.semaphore_signal(barrier, inc=1, device_id={axis: who}, device_id_type=MESH)

    for d in range(1, team):
        greet(base + lax.rem(place + d, team))

    @pl.when(jnp.logical_not(last))
    def _():
        greet(me + team)

        @pl.when(tail_place)
        def _():
            for p in range(team - 1):
                greet(base + team + p)

    @pl.when(jnp.logical_not(first))
    def _():
        greet(me - team)

        @pl.when(jnp.logical_not(tail_place))
        def _():
            greet(base - 1)

    ahead = jnp.where(tail_place, team, 1)
    behind = jnp.where(tail_place, 1, 2)
    pl.semaphore_wait(barrier, team - 1 + jnp.where(last, 0, ahead) + jnp.where(first, 0, behind))

    def remote(src, dst, send, recv, to):
        return pltpu.make_async_remote_copy(
            src_ref=src, dst_ref=dst, send_sem=send, recv_sem=recv, device_id={axis: to}, device_id_type=MESH
        )

    def exchange(d):
        to = lax.rem(place + d, team)
        pairs = [(src.at[:, lanes_of(to, width)], dst.at[rows_of(place), :]) for src, dst, width in streams]
        pairs += [(src, dst.at[place]) for src, dst in whole]
        return [
            remote(a, b, send_sem.at[d - 1, i], recv_sem.at[d - 1, i], base + to) for i, (a, b) in enumerate(pairs)
        ]

    def arrival(d):
        who = lax.rem(place + team - d, team)
        pairs = [(src.at[:, lanes_of(place, width)], dst.at[rows_of(who), :]) for src, dst, width in streams]
        pairs += [(src, dst.at[who]) for src, dst in whole]
        return [
            remote(a, b, send_sem.at[d - 1, i], recv_sem.at[d - 1, i], base + who) for i, (a, b) in enumerate(pairs)
        ]

    def rim(p, to):
        return [
            remote(
                src.at[pl.ds(rows - RIM, RIM), pl.ds(p * width, width)], dst.at[pl.ds(0, RIM), :],
                rim_send.at[p, i], rim_recv.at[i], to,
            )
            for i, (src, dst, width) in enumerate(streams)
        ]

    for d in range(1, team):
        for copy in exchange(d):
            copy.start()

    @pl.when(tail_place & jnp.logical_not(last))
    def _():
        for p in range(team):
            for copy in rim(p, base + team + p):
                copy.start()

    @pl.when(first)
    def _():
        for _, dst, _ in streams:
            dst[pl.ds(0, RIM), :] = jnp.zeros((RIM, dst.shape[1]), BF)
        held[...] = jnp.zeros_like(held)

    for copy in staying:
        copy.wait()

    @pl.when(jnp.logical_not(first))
    def _():
        for copy in rim(0, base - 1):
            copy.wait_recv()

    for d in range(1, team):
        for copy in arrival(d):
            copy.wait_recv()

    blocks = []
    for src, w_ref, f_ref, count in ((q_rows, wq, fq, kpm), (k_rows, wk, fk, kpm), (v_rows, wv, fv, hpm)):
        f_ref[...] = src[...].astype(F32)
        parts = []
        for b in range(team):
            for c in range(count):
                lanes = pl.ds(c * size, size)
                parts.append(
                    conv_silu(
                        lambda i: f_ref[pl.ds(RIM - taps + 1 + i + b * rows, rows), lanes], w_ref[:, lanes], rows
                    )
                )
        blocks.append(parts)
    qs, ks, vs = blocks

    heads = bl_ref.shape[0]
    diag = lax.broadcasted_iota(jnp.int32, (heads, heads), 0) == lax.broadcasted_iota(jnp.int32, (heads, heads), 1)

    def upright(ref):
        return jnp.sum(jnp.where(diag, ref[...], 0.0), axis=1, keepdims=True)

    scale_up, shift = jnp.exp(upright(al)), upright(dt)
    beta_rows, decay_rows = [], []
    for b in range(team):
        x = inputs[b] + shift
        decay = -scale_up * (jnp.maximum(x, 0.0) + jnp.log1p(jnp.exp(-jnp.abs(x))))
        beta = jax.nn.sigmoid(logits[b])
        for h in range(hpm):
            pick_b, pick_d = beta[h : h + 1], decay[h : h + 1]
            for p in range(1, team):
                at = p * hpm + h
                pick_b = jnp.where(place == p, beta[at : at + 1], pick_b)
                pick_d = jnp.where(place == p, decay[at : at + 1], pick_d)
            beta_rows.append(pick_b)
            decay_rows.append(pick_d)
    beta_rows = jnp.concatenate(beta_rows, axis=0)
    decay_rows = jnp.concatenate(decay_rows, axis=0)
    for u, (move, end, grow, reach, inside) in enumerate(block_maps(qs, ks, vs, beta_rows, decay_rows, repeat)):
        m_s[u] = move.astype(BF)
        g_s[pl.ds(u, 1), :] = end
        b_s[u] = grow
        p_s[u] = reach.astype(BF)
        o_s[u] = inside

    def hop(h, to):
        return remote(sent.at[h], held.at[h], hop_send.at[h], hop_recv.at[h], to)

    @pl.when(jnp.logical_not(first))
    def _():
        for h in range(hpm):
            hop(h, me - team).wait_recv()

    states = [held[h].astype(F32) for h in range(hpm)]
    starts = []
    for b in range(team):
        for h in range(hpm):
            u = b * hpm + h
            low = states[h].astype(BF)
            starts.append(low)
            states[h] = (
                b_s[u] + g_s[pl.ds(u, 1), :] * states[h] + jnp.dot(m_s[u], low, preferred_element_type=F32)
            )

    @pl.when(jnp.logical_not(last))
    def _():
        for h in range(hpm):
            sent[h] = states[h].astype(BF)
            hop(h, me + team).start()

    def home(b, to):
        return remote(back.at[b], out_ref.at[:, lanes_of(place, vw)], back_send.at[b], back_recv.at[place], to)

    for b in range(team):
        for h in range(hpm):
            u = b * hpm + h
            mixed = o_s[u] + jnp.dot(p_s[u], starts[u], preferred_element_type=F32)
            scale = lax.rsqrt(jnp.mean(mixed * mixed, axis=-1, keepdims=True) + 1e-06)
            back[b, :, pl.ds(h * size, size)] = (mixed * scale * gain[...]).astype(BF)

        @pl.when(place != b)
        def _():
            home(b, base + b).start()

        @pl.when(place == b)
        def _():
            out_ref[:, lanes_of(place, vw)] = back[b]

    for p in range(team):

        @pl.when(place != p)
        def _():
            remote(
                back.at[p], out_ref.at[:, pl.ds(p * vw, vw)], back_send.at[p], back_recv.at[p], base + p
            ).wait_recv()
            home(p, base + p).wait_send()

    for d in range(1, team):
        for copy in exchange(d):
            copy.wait_send()

    @pl.when(tail_place & jnp.logical_not(last))
    def _():
        for p in range(team):
            for copy in rim(p, base + team + p):
                copy.wait_send()

    @pl.when(jnp.logical_not(last))
    def _():
        for h in range(hpm):
            hop(h, me + team).wait_send()


def per_device(n, q_raw, k_raw, v_raw, gate_z, beta_logit, decay_in, conv_q, conv_k, conv_v, a_log, dt_bias, norm_gain):
    size = norm_gain.shape[0]
    rows, width = q_raw.shape
    vwidth = v_raw.shape[1]
    heads = vwidth // size
    taps = conv_q.shape[0]
    team = math.gcd(n, width // size)
    kw, vw = width // team, vwidth // team
    hpm = vw // size
    units = team * hpm
    long = RIM + team * rows
    dma = pltpu.SemaphoreType.DMA
    normed = pl.pallas_call(
        functools.partial(mixer_kernel, "context", n, team, size),
        out_shape=jax.ShapeDtypeStruct((rows, vwidth), BF),
        in_specs=[pl.BlockSpec(memory_space=pltpu.HBM)] * 11,
        out_specs=pl.BlockSpec(memory_space=pltpu.VMEM),
        scratch_shapes=[
            pltpu.VMEM((long, kw), BF),
            pltpu.VMEM((long, kw), BF),
            pltpu.VMEM((long, vw), BF),
            pltpu.VMEM((team, heads, rows), F32),
            pltpu.VMEM((team, heads, rows), F32),
            pltpu.VMEM((taps, kw), BF),
            pltpu.VMEM((taps, kw), BF),
            pltpu.VMEM((taps, vw), BF),
            pltpu.VMEM((1, heads), F32),
            pltpu.VMEM((1, heads), F32),
            pltpu.VMEM((1, size), F32),
            pltpu.VMEM((long, kw), F32),
            pltpu.VMEM((long, kw), F32),
            pltpu.VMEM((long, vw), F32),
            pltpu.VMEM((units, size, size), BF),
            pltpu.VMEM((units, size), F32),
            pltpu.VMEM((units, size, size), F32),
            pltpu.VMEM((units, rows, size), BF),
            pltpu.VMEM((units, rows, size), F32),
            pltpu.VMEM((hpm, size, size), BF),
            pltpu.VMEM((hpm, size, size), BF),
            pltpu.VMEM((team, rows, vw), BF),
            dma((11,)),
            dma((team, 5)),
            dma((team, 5)),
            dma((team, 3)),
            dma((3,)),
            dma((hpm,)),
            dma((hpm,)),
            dma((team,)),
            dma((team,)),
        ],
        compiler_params=pltpu.CompilerParams(
            collective_id=0, has_side_effects=True, vmem_limit_bytes=48 << 20
        ),
        name="mixer",
    )(
        q_raw, k_raw, v_raw, beta_logit.T, decay_in.T, conv_q, conv_k, conv_v,
        a_log[None], dt_bias[None], norm_gain[None],
    )
    return (normed.astype(F32) * jax.nn.silu(gate_z.astype(F32))).astype(BF)


def solution(mesh):
    rows = P(("groups", "context"), "tensor")
    return jax.shard_map(
        functools.partial(per_device, mesh.shape["context"]),
        mesh=mesh,
        in_specs=(rows,) * 6 + (P(None, "tensor"),) * 3 + (P("tensor"),) * 2 + (P(),),
        out_specs=rows,
        check_vma=False,
    )
```

time: 47.1 us -> 32.1 us (0.68)
  Pallas kernels: 36.9 us -> 23.7 us
  local copies, waits for them, and re-layouts: 9.58 us -> 6.86 us
  other arithmetic: 0 us -> 0.87 us
    pallas_call x3 -> x1, Pallas kernels: 36.9 us -> 23.7 us  [per_device(): pl.pallas_call(functools.partial(mixer_kernel, 'context', n, team, size),...]
    unnamed x39 -> x24, local copies, waits for them, and re-layouts: 9.58 us -> 6.86 us
    convert_element_type x0 -> x1, other arithmetic: none -> 0.87 us  [per_device(): return (normed.astype(F32) * jax.nn.silu(gate_z.astype(F32))).astype(BF)]
where the time goes in v2:
time: 32.1 us; the launch traced here: 31.5 us
  Pallas kernels  23.7 us (74%)
  local copies, waits for them, and re-layouts  6.86 us (21%)
  other arithmetic  0.87 us (3%)
    pallas_call x1, Pallas kernels, per_device(): pl.pallas_call(functools.partial(mixer_kernel, 'context', n, team, size),...  23.7 us
    unnamed x24, local copies, waits for them, and re-layouts  6.86 us
    convert_element_type x1, other arithmetic, per_device(): return (normed.astype(F32) * jax.nn.silu(gate_z.astype(F32))).astype(BF)  0.87 us

profile of v2, /device:TPU:26, one launch (start us, length us, event | category | flops | bytes accessed | tf_op | source)
XLA Modules:
  0.0 31.5 jit_solution(12562153502702442916)
XLA Ops:
  0.0 0.0 copy-start.3
  0.0 0.0 copy-start.8
  0.0 0.0 copy-start.9
  0.0 0.7 %copy-done.3 = bf16[4,1024]{1,0:T(4,128)(2,1)S(1)} copy-done((bf16[4,1024]{1,0:T(4,128)(2,1)S(1)}, bf16[4,1024]{1,0:T(4,128)(2,1)}, u32[]{:S(2)}) %copy-start.3) | copy-done | bytes 8216
  0.7 0.0 copy-done.8
  0.7 0.0 copy-done.9
  0.7 0.0 copy-start
  0.7 0.9 %copy-done = bf16[128,1024]{1,0:T(8,128)(2,1)S(1)} copy-done((bf16[128,1024]{1,0:T(8,128)(2,1)S(1)}, bf16[128,1024]{1,0:T(8,128)(2,1)}, u32[]{:S(2)}) %copy-start) | copy-done | bytes 262168
  1.7 0.0 copy-start.1
  1.7 0.9 %copy-done.1 = bf16[128,512]{1,0:T(8,128)(2,1)S(1)} copy-done((bf16[128,512]{1,0:T(8,128)(2,1)S(1)}, bf16[128,512]{1,0:T(8,128)(2,1)}, u32[]{:S(2)}) %copy-start.1) | copy-done | bytes 131096
  2.6 0.0 copy-start.2
  2.6 0.9 %copy-done.2 = bf16[128,512]{1,0:T(8,128)(2,1)S(1)} copy-done((bf16[128,512]{1,0:T(8,128)(2,1)S(1)}, bf16[128,512]{1,0:T(8,128)(2,1)}, u32[]{:S(2)}) %copy-start.2) | copy-done | bytes 131096
  3.5 0.0 copy-start.4
  3.5 0.7 %copy-done.4 = f32[128,8]{0,1:T(8,128)S(1)} copy-done((f32[128,8]{0,1:T(8,128)S(1)}, f32[128,8]{0,1:T(8,128)}, u32[]{:S(2)}) %copy-start.4) | copy-done | bytes 4120
  4.2 0.0 copy-start.5
  4.2 0.7 %copy-done.5 = f32[128,8]{0,1:T(8,128)S(1)} copy-done((f32[128,8]{0,1:T(8,128)S(1)}, f32[128,8]{0,1:T(8,128)}, u32[]{:S(2)}) %copy-start.5) | copy-done | bytes 4120
  4.8 0.0 copy-start.6
  4.8 0.7 %copy-done.6 = bf16[4,512]{1,0:T(4,128)(2,1)S(1)} copy-done((bf16[4,512]{1,0:T(4,128)(2,1)S(1)}, bf16[4,512]{1,0:T(4,128)(2,1)}, u32[]{:S(2)}) %copy-start.6) | copy-done | bytes 4120
  5.5 0.0 copy-start.7
  5.5 0.7 %copy-done.7 = bf16[4,512]{1,0:T(4,128)(2,1)S(1)} copy-done((bf16[4,512]{1,0:T(4,128)(2,1)S(1)}, bf16[4,512]{1,0:T(4,128)(2,1)}, u32[]{:S(2)}) %copy-start.7) | copy-done | bytes 4120
  6.2 0.0 copy-start.10
  6.2 0.7 %copy-done.10 = f32[128]{0:T(128)S(1)} copy-done((f32[128]{0:T(128)S(1)}, f32[128]{0:T(128)}, u32[]{:S(2)}) %copy-start.10) | copy-done | bytes 536
  6.9 0.0 copy-start.11
  6.9 23.7 %mixer.1 = bf16[128,1024]{1,0:T(8,128)(2,1)S(1)} custom-call(bf16[128,512]{1,0:T(8,128)(2,1)S(1)} %copy-done.1, bf16[128,512]{1,0:T(8,128)(2,1)S(1)} %copy-done.2, bf16[128,1024]{1,0:T(8,128)(2,1)S(1)} %copy-done, f32[8,128]{1,0:T(8,128)S(1)} %bitcast.5, f32[8,128]{1,0:T(8,128)S(1)} %bitcast.6, bf16[4,512]{1,0:T(4,128)(2,1)S(1)} %copy-done.6, ...), custom_call_target="tpu_custom_call" | custom-call | tf_op jit(solution)/shard_map/mixer/pallas_call | solution.py:349
  30.6 0.0 copy-done.11
  30.6 0.9 %fusion.4 = bf16[128,1024]{1,0:T(8,128)(2,1)} fusion(bf16[128,1024]{1,0:T(8,128)(2,1)S(1)} %copy-done.11, bf16[128,1024]{1,0:T(8,128)(2,1)S(1)} %mixer.1), kind=kLoop, calls=%fused_computation.6 | loop fusion | flops 1048576 | bytes 786432 | tf_op jit(solution)/shard_map/convert_element_type | solution.py:395
Async XLA Ops:
  0.0 0.7 %copy-start.3 = (bf16[4,1024]{1,0:T(4,128)(2,1)S(1)}, bf16[4,1024]{1,0:T(4,128)(2,1)}, u32[]{:S(2)}) copy-start(bf16[4,1024]{1,0:T(4,128)(2,1)} %wv_ref.1) | copy-start | bytes 24580
  0.0 0.7 %copy-start.8 = (f32[8]{0:T(128)S(1)}, f32[8]{0:T(128)}, u32[]{:S(2)}) copy-start(f32[8]{0:T(128)} %param.21) | copy-start | bytes 100
  0.0 0.7 %copy-start.9 = (f32[8]{0:T(128)S(1)}, f32[8]{0:T(128)}, u32[]{:S(2)}) copy-start(f32[8]{0:T(128)} %param.22) | copy-start | bytes 100
  0.7 1.0 %copy-start = (bf16[128,1024]{1,0:T(8,128)(2,1)S(1)}, bf16[128,1024]{1,0:T(8,128)(2,1)}, u32[]{:S(2)}) copy-start(bf16[128,1024]{1,0:T(8,128)(2,1)} %v_ref.1) | copy-start | bytes 786436
  1.7 0.9 %copy-start.1 = (bf16[128,512]{1,0:T(8,128)(2,1)S(1)}, bf16[128,512]{1,0:T(8,128)(2,1)}, u32[]{:S(2)}) copy-start(bf16[128,512]{1,0:T(8,128)(2,1)} %q_ref.1) | copy-start | bytes 393220
  2.6 0.9 %copy-start.2 = (bf16[128,512]{1,0:T(8,128)(2,1)S(1)}, bf16[128,512]{1,0:T(8,128)(2,1)}, u32[]{:S(2)}) copy-start(bf16[128,512]{1,0:T(8,128)(2,1)} %k_ref.1) | copy-start | bytes 393220
  3.5 0.7 %copy-start.4 = (f32[128,8]{0,1:T(8,128)S(1)}, f32[128,8]{0,1:T(8,128)}, u32[]{:S(2)}) copy-start(f32[128,8]{0,1:T(8,128)} %param.16) | copy-start | bytes 12292
  4.2 0.7 %copy-start.5 = (f32[128,8]{0,1:T(8,128)S(1)}, f32[128,8]{0,1:T(8,128)}, u32[]{:S(2)}) copy-start(f32[128,8]{0,1:T(8,128)} %param.17) | copy-start | bytes 12292
  4.8 0.7 %copy-start.6 = (bf16[4,512]{1,0:T(4,128)(2,1)S(1)}, bf16[4,512]{1,0:T(4,128)(2,1)}, u32[]{:S(2)}) copy-start(bf16[4,512]{1,0:T(4,128)(2,1)} %wq_ref.1) | copy-start | bytes 12292
  5.5 0.7 %copy-start.7 = (bf16[4,512]{1,0:T(4,128)(2,1)S(1)}, bf16[4,512]{1,0:T(4,128)(2,1)}, u32[]{:S(2)}) copy-start(bf16[4,512]{1,0:T(4,128)(2,1)} %wk_ref.1) | copy-start | bytes 12292
  6.2 0.7 %copy-start.10 = (f32[128]{0:T(128)S(1)}, f32[128]{0:T(128)}, u32[]{:S(2)}) copy-start(f32[128]{0:T(128)} %param.23) | copy-start | bytes 1540
  6.9 23.8 %copy-start.11 = (bf16[128,1024]{1,0:T(8,128)(2,1)S(1)}, bf16[128,1024]{1,0:T(8,128)(2,1)}, u32[]{:S(2)}) copy-start(bf16[128,1024]{1,0:T(8,128)(2,1)} %param.15) | copy-start | bytes 786436

commit v3 on v2

--- a/solution.py
+++ b/solution.py
@@ -35,38 +35,39 @@
     return (total * jax.nn.sigmoid(total)).astype(BF)
 
 
-def block_maps(qs, ks, vs, beta_rows, decay_rows, repeat):
-    rows, size = qs[0].shape
-    units = len(vs)
+def norm(block):
+    block = block.astype(F32)
+    return 1.0 / jnp.sqrt(jnp.sum(block * block, axis=-1, keepdims=True) + 1e-06)
+
+
+def masks(rows):
     row = lax.broadcasted_iota(jnp.int32, (rows, rows), 0)
     col = lax.broadcasted_iota(jnp.int32, (rows, rows), 1)
+    return row, col
+
+
+def key_stage(ks, beta_rows, decay_rows, repeat):
+    rows = ks[0].shape[0]
+    units = beta_rows.shape[0]
+    row, col = masks(rows)
     later = row >= col
     cum_rows = jnp.dot(decay_rows, (row <= col).astype(F32), precision=HIGH, preferred_element_type=F32)
     pad = jnp.zeros((rows - 2 * units, rows), F32)
     columns = jnp.concatenate([cum_rows, beta_rows, pad], axis=0).T
     cum, beta = columns[:, :units], columns[:, units : 2 * units]
-    growth = jnp.exp(cum)
-    tail = jnp.exp(cum[rows - 1 : rows] - cum)
-
-    def norm(block):
-        block = block.astype(F32)
-        return 1.0 / jnp.sqrt(jnp.sum(block * block, axis=-1, keepdims=True) + 1e-06)
-
-    qn = [norm(q) * size ** (-0.5) for q in qs]
     kn = [norm(k) for k in ks]
     kn_rows = jnp.zeros((rows, rows), F32)
     for j, column in enumerate(kn):
         kn_rows = jnp.where(col == j, column, kn_rows)
     kn_rows = kn_rows.T
     inner = [mm_nt(k, k) for k in ks]
-    cross = [mm_nt(q, k) for q, k in zip(qs, ks)]
-    lower, score = [], []
+    lower, ratios = [], []
     for h in range(units):
         j = h // repeat
         ratio = jnp.exp(jnp.minimum(cum[:, h : h + 1] - cum_rows[h : h + 1], 0.0))
         ratio = jnp.where(later, ratio, 0.0) * kn_rows[j : j + 1]
         lower.append(jnp.where(row > col, ratio * inner[j] * (beta[:, h : h + 1] * kn[j]), 0.0))
-        score.append((ratio * cross[j] * qn[j]).astype(BF))
+        ratios.append(ratio)
     eye = (row == col).astype(F32)
     inv = [eye - jnp.where(row // 2 == col // 2, m, 0.0) for m in lower]
     step = 2
@@ -75,24 +76,7 @@
         edge = [mm(jnp.where(mask, lower[h], 0.0), inv[h]) for h in range(units)]
         inv = [inv[h] - mm(inv[h], edge[h]) for h in range(units)]
         step *= 2
-    update, folded = [], []
-    for h in range(units):
-        j = h // repeat
-        beta_row = beta_rows[h : h + 1]
-        gain_row = beta_row * jnp.exp(cum_rows[h : h + 1]) * kn_rows[j : j + 1]
-        update.append(mm(inv[h] * beta_row, vs[h]).astype(BF))
-        folded.append(mm(inv[h] * gain_row, ks[j]).astype(BF))
-    result = []
-    for h in range(units):
-        j = h // repeat
-        key_tail = (ks[j].astype(F32) * (kn[j] * tail[:, h : h + 1])).astype(BF)
-        both = jnp.concatenate([folded[h], update[h]], axis=1)
-        ends = mm_tn(key_tail, both)
-        inside = mm(score[h], both)
-        reach = qs[j].astype(F32) * (qn[j] * growth[:, h : h + 1]) - inside[:, :size]
-        last = jnp.broadcast_to(growth[rows - 1 : rows, h : h + 1], (1, size))
-        result.append((-ends[:, :size], last, ends[:, size:], reach, inside[:, size:]))
-    return result
+    return cum, cum_rows, kn, kn_rows, ratios, inv
 
 
 def mixer_kernel(
@@ -100,7 +84,7 @@
     q_ref, k_ref, v_ref, bl_ref, di_ref, wq_ref, wk_ref, wv_ref, al_ref, dt_ref, gain_ref,
     out_ref,
     q_rows, k_rows, v_rows, logits, inputs, wq, wk, wv, al, dt, gain,
-    fq, fk, fv, m_s, g_s, b_s, p_s, o_s, held, sent, back,
+    fq, fk, fv, m_s, g_s, b_s, r_s, w_s, s_s, held, sent, back,
     local_sem, send_sem, recv_sem, rim_send, rim_recv, hop_send, hop_recv, back_send, back_recv,
 ):
     me = lax.axis_index(axis)
@@ -114,7 +98,8 @@
     units = team * hpm
     first, last = turn == 0, turn == n // team - 1
     tail_place = place == team - 1
-    streams = ((q_ref, q_rows, kw), (k_ref, k_rows, kw), (v_ref, v_rows, vw))
+    streams = ((k_ref, k_rows, kw), (v_ref, v_rows, vw), (q_ref, q_rows, kw))
+    plans = ((k_rows, wk, fk, kpm), (v_rows, wv, fv, hpm), (q_rows, wq, fq, kpm))
     whole = ((bl_ref, logits), (di_ref, inputs))
 
     def lanes_of(who, width):
@@ -185,24 +170,25 @@
             remote(a, b, send_sem.at[d - 1, i], recv_sem.at[d - 1, i], base + who) for i, (a, b) in enumerate(pairs)
         ]
 
-    def rim(p, to):
-        return [
-            remote(
-                src.at[pl.ds(rows - RIM, RIM), pl.ds(p * width, width)], dst.at[pl.ds(0, RIM), :],
-                rim_send.at[p, i], rim_recv.at[i], to,
-            )
-            for i, (src, dst, width) in enumerate(streams)
-        ]
-
-    for d in range(1, team):
-        for copy in exchange(d):
-            copy.start()
-
-    @pl.when(tail_place & jnp.logical_not(last))
-    def _():
-        for p in range(team):
-            for copy in rim(p, base + team + p):
-                copy.start()
+    def rim(p, to, i):
+        src, dst, width = streams[i]
+        return remote(
+            src.at[pl.ds(rows - RIM, RIM), pl.ds(p * width, width)], dst.at[pl.ds(0, RIM), :],
+            rim_send.at[p, i], rim_recv.at[i], to,
+        )
+
+    sends = [exchange(d) for d in range(1, team)]
+    takes = [arrival(d) for d in range(1, team)]
+    order = (3, 4, 0, 1, 2)
+    for i in order:
+        for copies in sends:
+            copies[i].start()
+        if i < len(streams):
+
+            @pl.when(tail_place & jnp.logical_not(last))
+            def _():
+                for p in range(team):
+                    rim(p, base + team + p, i).start()
 
     @pl.when(first)
     def _():
@@ -210,20 +196,22 @@
             dst[pl.ds(0, RIM), :] = jnp.zeros((RIM, dst.shape[1]), BF)
         held[...] = jnp.zeros_like(held)
 
-    for copy in staying:
+    for copy in staying[len(streams) :]:
         copy.wait()
-
-    @pl.when(jnp.logical_not(first))
-    def _():
-        for copy in rim(0, base - 1):
-            copy.wait_recv()
-
-    for d in range(1, team):
-        for copy in arrival(d):
-            copy.wait_recv()
-
-    blocks = []
-    for src, w_ref, f_ref, count in ((q_rows, wq, fq, kpm), (k_rows, wk, fk, kpm), (v_rows, wv, fv, hpm)):
+    for i in (3, 4):
+        for copies in takes:
+            copies[i].wait_recv()
+
+    def stream(i):
+        staying[i].wait()
+
+        @pl.when(jnp.logical_not(first))
+        def _():
+            rim(0, base - 1, i).wait_recv()
+
+        for copies in takes:
+            copies[i].wait_recv()
+        src, w_ref, f_ref, count = plans[i]
         f_ref[...] = src[...].astype(F32)
         parts = []
         for b in range(team):
@@ -234,8 +222,7 @@
                         lambda i: f_ref[pl.ds(RIM - taps + 1 + i + b * rows, rows), lanes], w_ref[:, lanes], rows
                     )
                 )
-        blocks.append(parts)
-    qs, ks, vs = blocks
+        return parts
 
     heads = bl_ref.shape[0]
     diag = lax.broadcasted_iota(jnp.int32, (heads, heads), 0) == lax.broadcasted_iota(jnp.int32, (heads, heads), 1)
@@ -259,45 +246,73 @@
             decay_rows.append(pick_d)
     beta_rows = jnp.concatenate(beta_rows, axis=0)
     decay_rows = jnp.concatenate(decay_rows, axis=0)
-    for u, (move, end, grow, reach, inside) in enumerate(block_maps(qs, ks, vs, beta_rows, decay_rows, repeat)):
-        m_s[u] = move.astype(BF)
-        g_s[pl.ds(u, 1), :] = end
-        b_s[u] = grow
-        p_s[u] = reach.astype(BF)
-        o_s[u] = inside
+    ks = stream(0)
+    cum, cum_rows, kn, kn_rows, ratios, inv = key_stage(ks, beta_rows, decay_rows, repeat)
+    growth = jnp.exp(cum)
+    tail = jnp.exp(cum[rows - 1 : rows] - cum)
+    for u in range(units):
+        r_s[u] = ratios[u]
+        beta_row = beta_rows[u : u + 1]
+        gain_row = beta_row * jnp.exp(cum_rows[u : u + 1]) * kn_rows[u // repeat : u // repeat + 1]
+        w_s[u, :, pl.ds(0, size)] = mm(inv[u] * gain_row, ks[u // repeat]).astype(BF)
+    inv = [(inv[u] * beta_rows[u : u + 1]).astype(BF) for u in range(units)]
+    vs = stream(1)
+    for u in range(units):
+        w_s[u, :, pl.ds(size, size)] = mm(inv[u], vs[u]).astype(BF)
+    for u in range(units):
+        key_tail = (ks[u // repeat].astype(F32) * (kn[u // repeat] * tail[:, u : u + 1])).astype(BF)
+        ends = mm_tn(key_tail, w_s[u])
+        m_s[u] = (-ends[:, :size]).astype(BF)
+        b_s[u] = ends[:, size:]
+        g_s[pl.ds(u, 1), :] = jnp.broadcast_to(growth[rows - 1 : rows, u : u + 1], (1, size))
 
     def hop(h, to):
         return remote(sent.at[h], held.at[h], hop_send.at[h], hop_recv.at[h], to)
 
+    def carry():
+        states = [held[h].astype(F32) for h in range(hpm)]
+        for b in range(team):
+            for h in range(hpm):
+                u = b * hpm + h
+                low = states[h].astype(BF)
+                s_s[u] = low
+                states[h] = (
+                    b_s[u] + g_s[pl.ds(u, 1), :] * states[h] + jnp.dot(m_s[u], low, preferred_element_type=F32)
+                )
+
+        @pl.when(jnp.logical_not(last))
+        def _():
+            for h in range(hpm):
+                sent[h] = states[h].astype(BF)
+                hop(h, me + team).start()
+
+    @pl.when(first)
+    def _():
+        carry()
+
+    qs = stream(2)
+    cross = [mm_nt(q, k) for q, k in zip(qs, ks)]
+    qn = [norm(q) * size ** (-0.5) for q in qs]
+    reach, within = [], []
+    for u in range(units):
+        j = u // repeat
+        inside = mm(r_s[u] * cross[j] * qn[j], w_s[u])
+        reach.append((qs[j].astype(F32) * (qn[j] * growth[:, u : u + 1]) - inside[:, :size]).astype(BF))
+        within.append(inside[:, size:])
+
     @pl.when(jnp.logical_not(first))
     def _():
         for h in range(hpm):
             hop(h, me - team).wait_recv()
-
-    states = [held[h].astype(F32) for h in range(hpm)]
-    starts = []
+        carry()
+
+    def home(b, to):
+        return remote(back.at[b], out_ref.at[:, lanes_of(place, vw)], back_send.at[b], back_recv.at[place], to)
+
     for b in range(team):
         for h in range(hpm):
             u = b * hpm + h
-            low = states[h].astype(BF)
-            starts.append(low)
-            states[h] = (
-                b_s[u] + g_s[pl.ds(u, 1), :] * states[h] + jnp.dot(m_s[u], low, preferred_element_type=F32)
-            )
-
-    @pl.when(jnp.logical_not(last))
-    def _():
-        for h in range(hpm):
-            sent[h] = states[h].astype(BF)
-            hop(h, me + team).start()
-
-    def home(b, to):
-        return remote(back.at[b], out_ref.at[:, lanes_of(place, vw)], back_send.at[b], back_recv.at[place], to)
-
-    for b in range(team):
-        for h in range(hpm):
-            u = b * hpm + h
-            mixed = o_s[u] + jnp.dot(p_s[u], starts[u], preferred_element_type=F32)
+            mixed = within[u] + jnp.dot(reach[u], s_s[u], preferred_element_type=F32)
             scale = lax.rsqrt(jnp.mean(mixed * mixed, axis=-1, keepdims=True) + 1e-06)
             back[b, :, pl.ds(h * size, size)] = (mixed * scale * gain[...]).astype(BF)
 
@@ -318,15 +333,15 @@
             ).wait_recv()
             home(p, base + p).wait_send()
 
-    for d in range(1, team):
-        for copy in exchange(d):
+    for copies in sends:
+        for copy in copies:
             copy.wait_send()
 
     @pl.when(tail_place & jnp.logical_not(last))
     def _():
         for p in range(team):
-            for copy in rim(p, base + team + p):
-                copy.wait_send()
+            for i in range(len(streams)):
+                rim(p, base + team + p, i).wait_send()
 
     @pl.when(jnp.logical_not(last))
     def _():
@@ -369,8 +384,9 @@
             pltpu.VMEM((units, size, size), BF),
             pltpu.VMEM((units, size), F32),
             pltpu.VMEM((units, size, size), F32),
-            pltpu.VMEM((units, rows, size), BF),
-            pltpu.VMEM((units, rows, size), F32),
+            pltpu.VMEM((units, rows, rows), F32),
+            pltpu.VMEM((units, rows, 2 * size), BF),
+            pltpu.VMEM((units, size, size), BF),
             pltpu.VMEM((hpm, size, size), BF),
             pltpu.VMEM((hpm, size, size), BF),
             pltpu.VMEM((team, rows, vw), BF),
@@ -385,7 +401,7 @@
             dma((team,)),
         ],
         compiler_params=pltpu.CompilerParams(
-            collective_id=0, has_side_effects=True, vmem_limit_bytes=48 << 20
+            collective_id=0, has_side_effects=True, vmem_limit_bytes=60 << 20
         ),
         name="mixer",
     )(

time: 32.1 us -> 23.9 us (0.74)
  local copies, waits for them, and re-layouts: 6.86 us -> 0.01 us
  Pallas kernels: 23.7 us -> 21.7 us
  other arithmetic: 0.87 us -> 1.82 us
    unnamed x24 -> x2, local copies, waits for them, and re-layouts: 6.86 us -> 0.01 us
    pallas_call x1, Pallas kernels: 23.7 us -> 21.7 us  [per_device(): pl.pallas_call(functools.partial(mixer_kernel, 'context', n, team, size),...]
    convert_element_type x1, other arithmetic: 0.87 us -> 1.82 us  [per_device(): return (normed.astype(F32) * jax.nn.silu(gate_z.astype(F32))).astype(BF)]
where the time goes in v3:
time: 23.9 us; the launch traced here: 23.5 us
  Pallas kernels  21.7 us (91%)
  other arithmetic  1.82 us (8%)
    pallas_call x1, Pallas kernels, per_device(): pl.pallas_call(functools.partial(mixer_kernel, 'context', n, team, size),...  21.7 us
    convert_element_type x1, other arithmetic, per_device(): return (normed.astype(F32) * jax.nn.silu(gate_z.astype(F32))).astype(BF)  1.82 us

profile of v3, /device:TPU:26, one launch (start us, length us, event | category | flops | bytes accessed | tf_op | source)
XLA Modules:
  0.0 23.5 jit_solution(10782721323320217703)
XLA Ops:
  0.0 0.0 copy-start
  0.0 21.7 %mixer.1 = bf16[128,1024]{1,0:T(8,128)(2,1)} custom-call(bf16[128,512]{1,0:T(8,128)(2,1)} %q_ref.1, bf16[128,512]{1,0:T(8,128)(2,1)} %k_ref.1, bf16[128,1024]{1,0:T(8,128)(2,1)} %v_ref.1, f32[8,128]{1,0:T(8,128)} %bitcast.5, f32[8,128]{1,0:T(8,128)} %bitcast.6, bf16[4,512]{1,0:T(4,128)(2,1)} %wq_ref.1, bf16[4,512]{1,0:T(4,128)(2,1)} %wk_ref.1, ...), custom_call_target="tpu_custom_call" | custom-call | tf_op jit(solution)/shard_map/mixer/pallas_call | solution.py:364
  21.7 0.0 copy-done
  21.7 1.8 %fusion.4 = bf16[128,1024]{1,0:T(8,128)(2,1)} fusion(bf16[128,1024]{1,0:T(8,128)(2,1)S(1)} %copy-done, bf16[128,1024]{1,0:T(8,128)(2,1)} %mixer.1), kind=kLoop, calls=%fused_computation.6 | loop fusion | flops 1048576 | bytes 786432 | tf_op jit(solution)/shard_map/convert_element_type | solution.py:411
Async XLA Ops:
  0.0 21.7 %copy-start = (bf16[128,1024]{1,0:T(8,128)(2,1)S(1)}, bf16[128,1024]{1,0:T(8,128)(2,1)}, u32[]{:S(2)}) copy-start(bf16[128,1024]{1,0:T(8,128)(2,1)} %param.15) | copy-start | bytes 786436

commit v4 on v3

--- a/solution.py
+++ b/solution.py
@@ -69,10 +69,11 @@
         lower.append(jnp.where(row > col, ratio * inner[j] * (beta[:, h : h + 1] * kn[j]), 0.0))
         ratios.append(ratio)
     eye = (row == col).astype(F32)
-    inv = [eye - jnp.where(row // 2 == col // 2, m, 0.0) for m in lower]
+    apart = row ^ col
+    inv = [eye - jnp.where(apart == 1, m, 0.0) for m in lower]
     step = 2
     while step < rows:
-        mask = (row // (2 * step) == col // (2 * step)) & (row // step != col // step)
+        mask = (apart >= step) & (apart < 2 * step)
         edge = [mm(jnp.where(mask, lower[h], 0.0), inv[h]) for h in range(units)]
         inv = [inv[h] - mm(inv[h], edge[h]) for h in range(units)]
         step *= 2
@@ -84,7 +85,7 @@
     q_ref, k_ref, v_ref, bl_ref, di_ref, wq_ref, wk_ref, wv_ref, al_ref, dt_ref, gain_ref,
     out_ref,
     q_rows, k_rows, v_rows, logits, inputs, wq, wk, wv, al, dt, gain,
-    fq, fk, fv, m_s, g_s, b_s, r_s, w_s, s_s, held, sent, back,
+    fq, fk, fv, m_s, g_s, b_s, r_s, w_s, s_s, p_s, o_s, held, sent, back,
     local_sem, send_sem, recv_sem, rim_send, rim_recv, hop_send, hop_recv, back_send, back_recv,
 ):
     me = lax.axis_index(axis)
@@ -194,7 +195,6 @@
     def _():
         for _, dst, _ in streams:
             dst[pl.ds(0, RIM), :] = jnp.zeros((RIM, dst.shape[1]), BF)
-        held[...] = jnp.zeros_like(held)
 
     for copy in staying[len(streams) :]:
         copy.wait()
@@ -269,9 +269,19 @@
     def hop(h, to):
         return remote(sent.at[h], held.at[h], hop_send.at[h], hop_recv.at[h], to)
 
-    def carry():
-        states = [held[h].astype(F32) for h in range(hpm)]
-        for b in range(team):
+    def onward(states):
+        @pl.when(jnp.logical_not(last))
+        def _():
+            for h in range(hpm):
+                sent[h] = states[h].astype(BF)
+                hop(h, me + team).start()
+
+    @pl.when(first)
+    def _():
+        states = [b_s[h] for h in range(hpm)]
+        for h in range(hpm):
+            s_s[h] = jnp.zeros((size, size), BF)
+        for b in range(1, team):
             for h in range(hpm):
                 u = b * hpm + h
                 low = states[h].astype(BF)
@@ -279,32 +289,46 @@
                 states[h] = (
                     b_s[u] + g_s[pl.ds(u, 1), :] * states[h] + jnp.dot(m_s[u], low, preferred_element_type=F32)
                 )
-
-        @pl.when(jnp.logical_not(last))
-        def _():
-            for h in range(hpm):
-                sent[h] = states[h].astype(BF)
-                hop(h, me + team).start()
-
-    @pl.when(first)
-    def _():
-        carry()
+        onward(states)
 
     qs = stream(2)
     cross = [mm_nt(q, k) for q, k in zip(qs, ks)]
     qn = [norm(q) * size ** (-0.5) for q in qs]
-    reach, within = [], []
     for u in range(units):
         j = u // repeat
         inside = mm(r_s[u] * cross[j] * qn[j], w_s[u])
-        reach.append((qs[j].astype(F32) * (qn[j] * growth[:, u : u + 1]) - inside[:, :size]).astype(BF))
-        within.append(inside[:, size:])
+        p_s[u] = (qs[j].astype(F32) * (qn[j] * growth[:, u : u + 1]) - inside[:, :size]).astype(BF)
+        o_s[u] = inside[:, size:]
 
     @pl.when(jnp.logical_not(first))
     def _():
+        row, col = masks(size)
+        eye = (row == col).astype(F32)
+        turns = [g_s[pl.ds(h, 1), :] * eye + m_s[h].astype(F32) for h in range(hpm)]
+        adds = [b_s[h] for h in range(hpm)]
+        for b in range(1, team):
+            for h in range(hpm):
+                u = b * hpm + h
+                low = jnp.concatenate([turns[h].astype(BF), adds[h].astype(BF)], axis=1)
+                end = g_s[pl.ds(u, 1), :]
+                moved = jnp.dot(m_s[u], low, preferred_element_type=F32)
+                seen = jnp.dot(p_s[u], low, preferred_element_type=F32)
+                p_s[u] = seen[:, :size].astype(BF)
+                o_s[u] = o_s[u] + seen[:, size:]
+                turns[h] = end * turns[h] + moved[:, :size]
+                adds[h] = b_s[u] + end * adds[h] + moved[:, size:]
+        for h in range(hpm):
+            m_s[h] = turns[h].astype(BF)
+            b_s[h] = adds[h]
         for h in range(hpm):
             hop(h, me - team).wait_recv()
-        carry()
+
+        @pl.when(jnp.logical_not(last))
+        def _():
+            onward([b_s[h] + jnp.dot(m_s[h], held[h], preferred_element_type=F32) for h in range(hpm)])
+
+        for u in range(units):
+            s_s[u] = held[u % hpm]
 
     def home(b, to):
         return remote(back.at[b], out_ref.at[:, lanes_of(place, vw)], back_send.at[b], back_recv.at[place], to)
@@ -312,7 +336,7 @@
     for b in range(team):
         for h in range(hpm):
             u = b * hpm + h
-            mixed = within[u] + jnp.dot(reach[u], s_s[u], preferred_element_type=F32)
+            mixed = o_s[u] + jnp.dot(p_s[u], s_s[u], preferred_element_type=F32)
             scale = lax.rsqrt(jnp.mean(mixed * mixed, axis=-1, keepdims=True) + 1e-06)
             back[b, :, pl.ds(h * size, size)] = (mixed * scale * gain[...]).astype(BF)
 
@@ -387,6 +411,8 @@
             pltpu.VMEM((units, rows, rows), F32),
             pltpu.VMEM((units, rows, 2 * size), BF),
             pltpu.VMEM((units, size, size), BF),
+            pltpu.VMEM((units, rows, size), BF),
+            pltpu.VMEM((units, rows, size), F32),
             pltpu.VMEM((hpm, size, size), BF),
             pltpu.VMEM((hpm, size, size), BF),
             pltpu.VMEM((team, rows, vw), BF),

time: 23.9 us -> 23.3 us (0.975)
  Pallas kernels: 21.7 us -> 21.1 us
    pallas_call x1, Pallas kernels: 21.7 us -> 21.1 us  [per_device(): pl.pallas_call(functools.partial(mixer_kernel, 'context', n, team, size),...]
where the time goes in v4:
time: 23.3 us; the launch traced here: 22.9 us
  Pallas kernels  21.1 us (91%)
  other arithmetic  1.82 us (8%)
    pallas_call x1, Pallas kernels, per_device(): pl.pallas_call(functools.partial(mixer_kernel, 'context', n, team, size),...  21.1 us
    convert_element_type x1, other arithmetic, per_device(): return (normed.astype(F32) * jax.nn.silu(gate_z.astype(F32))).astype(BF)  1.82 us

profile of v4, /device:TPU:26, one launch (start us, length us, event | category | flops | bytes accessed | tf_op | source)
XLA Modules:
  0.0 22.9 jit_solution(16777898119057088884)
XLA Ops:
  0.0 0.0 copy-start
  0.0 21.1 %mixer.1 = bf16[128,1024]{1,0:T(8,128)(2,1)} custom-call(bf16[128,512]{1,0:T(8,128)(2,1)} %q_ref.1, bf16[128,512]{1,0:T(8,128)(2,1)} %k_ref.1, bf16[128,1024]{1,0:T(8,128)(2,1)} %v_ref.1, f32[8,128]{1,0:T(8,128)} %bitcast.5, f32[8,128]{1,0:T(8,128)} %bitcast.6, bf16[4,512]{1,0:T(4,128)(2,1)} %wq_ref.1, bf16[4,512]{1,0:T(4,128)(2,1)} %wk_ref.1, ...), custom_call_target="tpu_custom_call" | custom-call | tf_op jit(solution)/shard_map/mixer/pallas_call | solution.py:388
  21.1 0.0 copy-done
  21.1 1.8 %fusion.4 = bf16[128,1024]{1,0:T(8,128)(2,1)} fusion(bf16[128,1024]{1,0:T(8,128)(2,1)S(1)} %copy-done, bf16[128,1024]{1,0:T(8,128)(2,1)} %mixer.1), kind=kLoop, calls=%fused_computation.6 | loop fusion | flops 1048576 | bytes 786432 | tf_op jit(solution)/shard_map/convert_element_type | solution.py:437
Async XLA Ops:
  0.0 21.1 %copy-start = (bf16[128,1024]{1,0:T(8,128)(2,1)S(1)}, bf16[128,1024]{1,0:T(8,128)(2,1)}, u32[]{:S(2)}) copy-start(bf16[128,1024]{1,0:T(8,128)(2,1)} %param.15) | copy-start | bytes 786436

commit v5 on v4

--- a/solution.py
+++ b/solution.py
@@ -46,15 +46,19 @@
     return row, col
 
 
-def key_stage(ks, beta_rows, decay_rows, repeat):
-    rows = ks[0].shape[0]
-    units = beta_rows.shape[0]
+def decay_stage(beta_rows, decay_rows):
+    units, rows = beta_rows.shape
     row, col = masks(rows)
-    later = row >= col
     cum_rows = jnp.dot(decay_rows, (row <= col).astype(F32), precision=HIGH, preferred_element_type=F32)
     pad = jnp.zeros((rows - 2 * units, rows), F32)
     columns = jnp.concatenate([cum_rows, beta_rows, pad], axis=0).T
-    cum, beta = columns[:, :units], columns[:, units : 2 * units]
+    return cum_rows, columns[:, :units], columns[:, units : 2 * units]
+
+
+def key_stage(ks, beta, decays, repeat):
+    rows = ks[0].shape[0]
+    units = beta.shape[1]
+    row, col = masks(rows)
     kn = [norm(k) for k in ks]
     kn_rows = jnp.zeros((rows, rows), F32)
     for j, column in enumerate(kn):
@@ -64,8 +68,7 @@
     lower, ratios = [], []
     for h in range(units):
         j = h // repeat
-        ratio = jnp.exp(jnp.minimum(cum[:, h : h + 1] - cum_rows[h : h + 1], 0.0))
-        ratio = jnp.where(later, ratio, 0.0) * kn_rows[j : j + 1]
+        ratio = decays[h] * kn_rows[j : j + 1]
         lower.append(jnp.where(row > col, ratio * inner[j] * (beta[:, h : h + 1] * kn[j]), 0.0))
         ratios.append(ratio)
     eye = (row == col).astype(F32)
@@ -77,7 +80,7 @@
         edge = [mm(jnp.where(mask, lower[h], 0.0), inv[h]) for h in range(units)]
         inv = [inv[h] - mm(inv[h], edge[h]) for h in range(units)]
         step *= 2
-    return cum, cum_rows, kn, kn_rows, ratios, inv
+    return kn, kn_rows, ratios, inv
 
 
 def mixer_kernel(
@@ -246,10 +249,15 @@
             decay_rows.append(pick_d)
     beta_rows = jnp.concatenate(beta_rows, axis=0)
     decay_rows = jnp.concatenate(decay_rows, axis=0)
-    ks = stream(0)
-    cum, cum_rows, kn, kn_rows, ratios, inv = key_stage(ks, beta_rows, decay_rows, repeat)
+    cum_rows, cum, beta = decay_stage(beta_rows, decay_rows)
     growth = jnp.exp(cum)
     tail = jnp.exp(cum[rows - 1 : rows] - cum)
+    row, col = masks(rows)
+    for u in range(units):
+        ratio = jnp.exp(jnp.minimum(cum[:, u : u + 1] - cum_rows[u : u + 1], 0.0))
+        r_s[u] = jnp.where(row >= col, ratio, 0.0)
+    ks = stream(0)
+    kn, kn_rows, ratios, inv = key_stage(ks, beta, [r_s[u] for u in range(units)], repeat)
     for u in range(units):
         r_s[u] = ratios[u]
         beta_row = beta_rows[u : u + 1]
@@ -346,7 +354,7 @@
 
         @pl.when(place == b)
         def _():
-            out_ref[:, lanes_of(place, vw)] = back[b]
+            pltpu.make_async_copy(back.at[b], out_ref.at[:, lanes_of(place, vw)], back_recv.at[place]).start()
 
     for p in range(team):
 
@@ -356,6 +364,10 @@
                 back.at[p], out_ref.at[:, pl.ds(p * vw, vw)], back_send.at[p], back_recv.at[p], base + p
             ).wait_recv()
             home(p, base + p).wait_send()
+
+        @pl.when(place == p)
+        def _():
+            pltpu.make_async_copy(back.at[p], out_ref.at[:, lanes_of(place, vw)], back_recv.at[place]).wait()
 
     for copies in sends:
         for copy in copies:
@@ -389,7 +401,7 @@
         functools.partial(mixer_kernel, "context", n, team, size),
         out_shape=jax.ShapeDtypeStruct((rows, vwidth), BF),
         in_specs=[pl.BlockSpec(memory_space=pltpu.HBM)] * 11,
-        out_specs=pl.BlockSpec(memory_space=pltpu.VMEM),
+        out_specs=pl.BlockSpec(memory_space=pltpu.HBM),
         scratch_shapes=[
             pltpu.VMEM((long, kw), BF),
             pltpu.VMEM((long, kw), BF),

time: 23.3 us -> 21.9 us (0.940)
  Pallas kernels: 21.1 us -> 19.9 us
    pallas_call x1, Pallas kernels: 21.1 us -> 19.9 us  [per_device(): pl.pallas_call(functools.partial(mixer_kernel, 'context', n, team, size),...]
where the time goes in v5:
time: 21.9 us; the launch traced here: 21.7 us
  Pallas kernels  19.9 us (91%)
  other arithmetic  1.82 us (8%)
    pallas_call x1, Pallas kernels, per_device(): pl.pallas_call(functools.partial(mixer_kernel, 'context', n, team, size),...  19.9 us
    convert_element_type x1, other arithmetic, per_device(): return (normed.astype(F32) * jax.nn.silu(gate_z.astype(F32))).astype(BF)  1.82 us

profile of v5, /device:TPU:26, one launch (start us, length us, event | category | flops | bytes accessed | tf_op | source)
XLA Modules:
  0.0 21.7 jit_solution(8801724782908306930)
XLA Ops:
  0.0 0.0 copy-start
  0.0 19.9 %mixer.1 = bf16[128,1024]{1,0:T(8,128)(2,1)} custom-call(bf16[128,512]{1,0:T(8,128)(2,1)} %q_ref.1, bf16[128,512]{1,0:T(8,128)(2,1)} %k_ref.1, bf16[128,1024]{1,0:T(8,128)(2,1)} %v_ref.1, f32[8,128]{1,0:T(8,128)} %bitcast.5, f32[8,128]{1,0:T(8,128)} %bitcast.6, bf16[4,512]{1,0:T(4,128)(2,1)} %wq_ref.1, bf16[4,512]{1,0:T(4,128)(2,1)} %wk_ref.1, ...), custom_call_target="tpu_custom_call" | custom-call | tf_op jit(solution)/shard_map/mixer/pallas_call | solution.py:400
  19.9 0.0 copy-done
  19.9 1.8 %fusion.4 = bf16[128,1024]{1,0:T(8,128)(2,1)} fusion(bf16[128,1024]{1,0:T(8,128)(2,1)S(1)} %copy-done, bf16[128,1024]{1,0:T(8,128)(2,1)} %mixer.1), kind=kLoop, calls=%fused_computation.6 | loop fusion | flops 1048576 | bytes 786432 | tf_op jit(solution)/shard_map/convert_element_type | solution.py:449
Async XLA Ops:
  0.0 19.9 %copy-start = (bf16[128,1024]{1,0:T(8,128)(2,1)S(1)}, bf16[128,1024]{1,0:T(8,128)(2,1)}, u32[]{:S(2)}) copy-start(bf16[128,1024]{1,0:T(8,128)(2,1)} %param.15) | copy-start | bytes 786436
